TPU v7x, 32 devices: a whole 2x2x4 slice. The times are simulated.
32 devices in a mesh: dp: 8 (over y, x, core), tensor: 4 (over z).
Axes of the slice: x: 2, y: 2, z: 4, core: 2. Of those that a mesh axis runs over, the one named last changes fastest.
Arguments:
- tokens: bfloat16 [4096, 1536], P('dp'), may hold values from -6 to 6
- cotangent: bfloat16 [4096, 1536], P('dp'), may hold values from -6 to 6
- lengths: int32 [8, 4], P('dp'), may hold values from 1 to 256, 512 in all within a row
- gate_weight: float32 [1536, 3072], P('dp', 'tensor'), may hold values from -0.15625 to 0.15625
- inner_weight: float32 [1536, 3072], P('dp', 'tensor'), may hold values from -0.15625 to 0.15625
- output_weight: float32 [1536, 3072], P('dp', 'tensor'), may hold values from -0.109375 to 0.109375
- delta_weight: float32 [1536, 48], P('dp', 'tensor'), may hold values from -0.15625 to 0.15625
- state_weight: float32 [1536, 256], P('dp'), may hold values from -0.15625 to 0.15625
- inner_filter: float32 [5, 3072], P(None, 'tensor'), may hold values from -0.5 to 0.5
- state_filter: float32 [5, 256], replicated, may hold values from -0.5 to 0.5
- head_scalars: float32 [3, 48], P(None, 'tensor'), may hold values from -7 to 2, as said below
- norm_gain: float32 [3072], P('tensor'), may hold values from 0.5 to 1.5
- input_gain: float32 [1536], replicated, may hold values from 0.5 to 1.5
- gate_moment: float32 [1536, 3072], P('dp', 'tensor'), may hold values from -64 to 64
- inner_moment: float32 [1536, 3072], P('dp', 'tensor'), may hold values from -64 to 64
- output_moment: float32 [1536, 3072], P('dp', 'tensor'), may hold values from -64 to 64
- delta_moment: float32 [1536, 48], P('dp', 'tensor'), may hold values from -32 to 32
- state_moment: float32 [1536, 256], P('dp'), may hold values from -32 to 32
- inner_filter_moment: float32 [5, 3072], P(None, 'tensor'), may hold values from -64 to 64
- state_filter_moment: float32 [5, 256], replicated, may hold values from -64 to 64
- head_scalars_moment: float32 [3, 48], P(None, 'tensor'), may hold values from -64 to 64
- norm_gain_moment: float32 [3072], P('tensor'), may hold values from -64 to 64
- input_gain_moment: float32 [1536], replicated, may hold values from -64 to 64
Outputs:
- block_output: bfloat16 [4096, 1536], P('dp')
- input_gradient: float32 [4096, 1536], P('dp')
- gate_gradient: float32 [1536, 3072], P('dp', 'tensor')
- inner_gradient: float32 [1536, 3072], P('dp', 'tensor')
- output_gradient: float32 [1536, 3072], P('dp', 'tensor')
- delta_gradient: float32 [1536, 48], P('dp', 'tensor')
- state_gradient: float32 [1536, 256], P('dp')
- inner_filter_gradient: float32 [5, 3072], P(None, 'tensor')
- state_filter_gradient: float32 [5, 256], replicated
- head_scalars_gradient: float32 [3, 48], P(None, 'tensor')
- norm_gain_gradient: float32 [3072], P('tensor')
- input_gain_gradient: float32 [1536], replicated
- gate_updated: float32 [1536, 3072], P('dp', 'tensor')
- inner_updated: float32 [1536, 3072], P('dp', 'tensor')
- output_updated: float32 [1536, 3072], P('dp', 'tensor')
- delta_updated: float32 [1536, 48], P('dp', 'tensor')
- state_updated: float32 [1536, 256], P('dp')
- inner_filter_updated: float32 [5, 3072], P(None, 'tensor')
- state_filter_updated: float32 [5, 256], replicated
- head_scalars_updated: float32 [3, 48], P(None, 'tensor')
- norm_gain_updated: float32 [3072], P('tensor')
- input_gain_updated: float32 [1536], replicated
- gate_moment_new: float32 [1536, 3072], P('dp', 'tensor')
- inner_moment_new: float32 [1536, 3072], P('dp', 'tensor')
- output_moment_new: float32 [1536, 3072], P('dp', 'tensor')
- delta_moment_new: float32 [1536, 48], P('dp', 'tensor')
- state_moment_new: float32 [1536, 256], P('dp')
- inner_filter_moment_new: float32 [5, 3072], P(None, 'tensor')
- state_filter_moment_new: float32 [5, 256], replicated
- head_scalars_moment_new: float32 [3, 48], P(None, 'tensor')
- norm_gain_moment_new: float32 [3072], P('tensor')
- input_gain_moment_new: float32 [1536], replicated
Inputs may be any that keep to these rules, and one draw needn't show every extreme that they name: Each row holds the lengths of the 4 sequences packed in order into one device's 512 tokens; they sum to 512 and the largest is exactly 256. `head_scalars`: row 0 holds offsets of the step sizes, row 1 logarithms of decay rates, row 2 skip weights.
All inputs are finite; a program needn't handle non-finite values.
Results may differ from a plain program's by a relative error of at most 0.008.
The roundings to bfloat16 on the way count: a program that leaves them out, or rounds other values in their place, can miss the bound.
Values may be sent and summed in bfloat16 or wider, within the bound.
No kernel may reach another device: no remote copies, remote signals or barrier semaphores. Data moves between devices by JAX's collectives and lax.ppermute only.
A program may use at most 192 MiB of HBM per device.

v0:
```python
import math

import jax
import jax.numpy as jnp
from jax import lax
from jax.sharding import PartitionSpec as P

D = 1536
INNER = 3072
NSTATE = 128
CONV = 4
SPAN = 256
SCHULZ = 5


norm_epsilon = 1e-05
moment_decay = 0.95
muon_rate = 0.02
plain_rate = 0.002
schulz_terms = (3.4445, -4.775, 2.0315)
exact_mode = lax.Precision.HIGHEST


def broadcast(block, axis, holder):
    block = jnp.where(lax.axis_index(axis) == holder, block, jnp.zeros_like(block))
    return lax.psum(block, axis)


def packing_layout(length_row, row_count):
    ends = jnp.cumsum(length_row)
    places = jnp.arange(row_count, dtype=jnp.int32)
    after = (places[:, None] >= ends[None, :]).astype(jnp.int32)
    segment = jnp.sum(after, axis=1)
    starts = jnp.sum(after * length_row[None, :], axis=1)
    return (segment, places - starts)


def shifted_rows(values, offset):
    padding = jnp.zeros((offset, values.shape[1]), values.dtype)
    return jnp.concatenate([padding, values[: values.shape[0] - offset]], axis=0)


def causal_filter(values, taps, position):
    summed = taps[CONV] + taps[CONV - 1] * values
    for offset in range(1, CONV):
        inside = (position >= offset).astype(jnp.float32)[:, None]
        summed = summed + taps[CONV - 1 - offset] * shifted_rows(values, offset) * inside
    return jax.nn.silu(summed)


def state_mixer(
    gate_part,
    inner_part,
    delta_raw,
    entry_rows,
    readout_rows,
    inner_filter,
    head_scalars,
    segment,
    position,
):
    row_count, head_count = delta_raw.shape
    head_width = inner_part.shape[1] // head_count
    block_count = row_count // SPAN
    filtered = causal_filter(inner_part, inner_filter, position)
    delta_step = jax.nn.softplus(delta_raw + head_scalars[0])
    step_log = delta_step * -jnp.exp(head_scalars[1])
    heads_in = filtered.reshape(row_count, head_count, head_width)
    driven = (heads_in * delta_step[:, :, None]).reshape(block_count, SPAN, head_count, head_width)
    lower_mask = (jnp.arange(SPAN)[:, None] >= jnp.arange(SPAN)[None, :]).astype(jnp.float32)
    running = jnp.einsum(
        "ij,cjh->cih",
        lower_mask,
        step_log.reshape(block_count, SPAN, head_count),
        precision=exact_mode,
    )
    block_seg = segment.reshape(block_count, SPAN)
    same_seq = (block_seg[:, :, None] == block_seg[:, None, :]).astype(jnp.float32) * lower_mask
    spread = running[:, :, None, :] - running[:, None, :, :]
    entry_blocks = entry_rows.reshape(block_count, SPAN, -1)
    readout_blocks = readout_rows.reshape(block_count, SPAN, -1)
    correlation = jnp.einsum("cin,cjn->cij", readout_blocks, entry_blocks, precision=exact_mode)
    mixing = jnp.exp(jnp.minimum(spread, 0.0)) * (correlation * same_seq)[:, :, :, None]
    within = jnp.einsum("cijh,cjhp->cihp", mixing, driven, precision=exact_mode)
    final_log = running[:, -1, :]
    last_seg = block_seg[:, -1]
    tail_weight = (
        jnp.exp(final_log[:, None, :] - running)
        * (block_seg == last_seg[:, None]).astype(jnp.float32)[:, :, None]
    )
    fresh_states = jnp.einsum(
        "cjh,cjhp,cjn->chpn", tail_weight, driven, entry_blocks, precision=exact_mode
    )
    prior_seg = jnp.concatenate([jnp.full((1,), -1, dtype=jnp.int32), last_seg[:-1]])
    carry_keep = (last_seg == prior_seg).astype(jnp.float32)

    def advance(carried_state, pieces):
        keep_flag, total_log, update = pieces
        return (
            keep_flag * jnp.exp(total_log)[:, None, None] * carried_state + update,
            carried_state,
        )

    start_state = jnp.zeros(fresh_states.shape[1:], jnp.float32)
    final_state, entering = lax.scan(advance, start_state, (carry_keep, final_log, fresh_states))
    reach_weight = (
        jnp.exp(running) * (block_seg == prior_seg[:, None]).astype(jnp.float32)[:, :, None]
    )
    carried = jnp.einsum(
        "cih,cin,chpn->cihp", reach_weight, readout_blocks, entering, precision=exact_mode
    )
    outputs = (within + carried).reshape(row_count, head_count, head_width) + head_scalars[2][
        None, :, None
    ] * heads_in
    return outputs.reshape(row_count, head_count * head_width) * jax.nn.silu(gate_part)


def tensor_total(values):
    return lax.psum(values, "tensor")


def owner_schulz(rounded):
    widened = rounded.astype(jnp.float32)
    frobenius = jnp.sqrt(tensor_total(jnp.sum(widened * widened)))
    iterate = (widened / (frobenius + 1e-07)).astype(jnp.bfloat16)
    for sweep in range(SCHULZ):
        gram_matrix = tensor_total(jnp.dot(iterate, iterate.T, preferred_element_type=jnp.float32))
        gram_low = gram_matrix.astype(jnp.bfloat16)
        squared = jnp.dot(gram_low, gram_low, preferred_element_type=jnp.float32)
        polynomial = (schulz_terms[1] * gram_matrix + schulz_terms[2] * squared).astype(
            jnp.bfloat16
        )
        iterate = (
            schulz_terms[0] * iterate.astype(jnp.float32)
            + jnp.dot(polynomial, iterate, preferred_element_type=jnp.float32)
        ).astype(jnp.bfloat16)
    return iterate


def plain_update(weight, moment, gradient):
    fresh = moment_decay * moment + gradient
    return (weight - plain_rate * fresh, fresh)


def local(
    tokens,
    cotangent,
    lengths,
    gate_weight,
    inner_weight,
    output_weight,
    delta_weight,
    state_weight,
    inner_filter,
    state_filter,
    head_scalars,
    norm_gain,
    input_gain,
    gate_moment,
    inner_moment,
    output_moment,
    delta_moment,
    state_moment,
    inner_filter_moment,
    state_filter_moment,
    head_scalars_moment,
    norm_gain_moment,
    input_gain_moment,
):
    row_count = tokens.shape[0]
    segment, position = packing_layout(lengths[0], row_count)
    full_gate, full_inner, full_output, full_delta, full_state = (
        lax.all_gather(gate_weight.astype(jnp.bfloat16), "dp", axis=0, tiled=True),
        lax.all_gather(inner_weight.astype(jnp.bfloat16), "dp", axis=0, tiled=True),
        lax.all_gather(output_weight.astype(jnp.bfloat16), "dp", axis=0, tiled=True),
        lax.all_gather(delta_weight.astype(jnp.bfloat16), "dp", axis=0, tiled=True),
        lax.all_gather(state_weight.astype(jnp.bfloat16), "dp", axis=0, tiled=True),
    )
    columns = full_gate.shape[1]
    head_count = full_delta.shape[1]
    mixing_cols = 2 * columns + head_count
    in_matrix = jnp.concatenate([full_gate, full_inner, full_delta, full_state], axis=1)
    tokens_wide = tokens.astype(jnp.float32)
    root_scale = lax.rsqrt(
        jnp.mean(tokens_wide * tokens_wide, axis=1, keepdims=True) + norm_epsilon
    )
    normed = (tokens_wide * root_scale * input_gain).astype(jnp.bfloat16)
    projected = jnp.dot(normed, in_matrix, preferred_element_type=jnp.float32)
    gate_part = projected[:, :columns]
    inner_part = projected[:, columns : 2 * columns]
    delta_raw = projected[:, 2 * columns : mixing_cols]
    state_raw = projected[:, mixing_cols:]

    def state_rows(raw_values, taps):
        filtered = causal_filter(raw_values, taps, position)
        return (filtered[:, :NSTATE], filtered[:, NSTATE:])

    def mixer(gate_in, inner_in, delta_in, entry_in, readout_in, taps, scalars):
        return state_mixer(
            gate_in, inner_in, delta_in, entry_in, readout_in, taps, scalars, segment, position
        )

    (entry_rows, readout_rows), state_back = jax.vjp(state_rows, state_raw, state_filter)
    gated, mixer_back = jax.vjp(
        mixer,
        gate_part,
        inner_part,
        delta_raw,
        entry_rows,
        readout_rows,
        inner_filter,
        head_scalars,
    )
    squares = lax.psum(jnp.sum(gated * gated, axis=1), "tensor")
    norm_scale = lax.rsqrt(squares / INNER + norm_epsilon)[:, None]
    normalized = (gated * norm_scale * norm_gain).astype(jnp.bfloat16)
    partial_out = jnp.einsum(
        "ti,di->td", normalized, full_output, preferred_element_type=jnp.float32
    )
    block_output = (tokens_wide + lax.psum(partial_out, "tensor")).astype(jnp.bfloat16)
    grad_normalized = jnp.dot(cotangent, full_output, preferred_element_type=jnp.float32)
    output_local = jnp.einsum(
        "td,ti->di", cotangent, normalized, preferred_element_type=jnp.float32
    )
    norm_gain_local = jnp.sum(grad_normalized * gated * norm_scale, axis=0)
    weighted = grad_normalized * norm_gain
    inner_dot = lax.psum(jnp.sum(weighted * gated, axis=1), "tensor")
    grad_gated = norm_scale * weighted - gated * norm_scale**3 * (inner_dot / INNER)[:, None]
    grad_gate, grad_inner, grad_delta, grad_entry, grad_readout, filter_local, scalar_local = (
        mixer_back(grad_gated)
    )
    entry_total, readout_total = lax.psum((grad_entry, grad_readout), "tensor")
    grad_state, state_filter_local = state_back((entry_total, readout_total))
    grad_mixing = jnp.concatenate([grad_gate, grad_inner, grad_delta], axis=1).astype(jnp.bfloat16)
    grad_state_low = grad_state.astype(jnp.bfloat16)
    input_partial = jnp.einsum(
        "tk,dk->td", grad_mixing, in_matrix[:, :mixing_cols], preferred_element_type=jnp.float32
    )
    mixing_weight_grad = jnp.einsum(
        "td,tk->dk", normed, grad_mixing, preferred_element_type=jnp.float32
    )
    state_local = jnp.einsum(
        "td,tk->dk", normed, grad_state_low, preferred_element_type=jnp.float32
    )
    state_input = jnp.einsum(
        "tk,dk->td", grad_state_low, full_state, preferred_element_type=jnp.float32
    )
    grad_normed = lax.psum(input_partial, "tensor") + state_input
    input_gain_local = jnp.sum(grad_normed * tokens_wide * root_scale, axis=0)
    weighted_in = grad_normed * input_gain
    row_mean = jnp.mean(weighted_in * tokens_wide, axis=1, keepdims=True)
    input_gradient = (
        cotangent.astype(jnp.float32)
        + root_scale * weighted_in
        - tokens_wide * root_scale**3 * row_mean
    )
    gate_sum, inner_sum, output_sum, delta_sum, state_sum = (
        lax.psum_scatter(mixing_weight_grad[:, :columns], "dp", scatter_dimension=0, tiled=True),
        lax.psum_scatter(
            mixing_weight_grad[:, columns : 2 * columns], "dp", scatter_dimension=0, tiled=True
        ),
        lax.psum_scatter(output_local, "dp", scatter_dimension=0, tiled=True),
        lax.psum_scatter(
            mixing_weight_grad[:, 2 * columns :], "dp", scatter_dimension=0, tiled=True
        ),
        lax.psum_scatter(state_local, "dp", scatter_dimension=0, tiled=True),
    )
    filter_sum, state_filter_sum, scalar_sum, norm_gain_sum, input_gain_sum = lax.psum(
        (filter_local, state_filter_local, scalar_local, norm_gain_local, input_gain_local), "dp"
    )
    fresh_stack = moment_decay * jnp.stack([gate_moment, inner_moment, output_moment]) + jnp.stack(
        [gate_sum, inner_sum, output_sum]
    )
    rounded_stack = fresh_stack.astype(jnp.bfloat16)
    local_rows = rounded_stack.shape[1]
    axis_count = lax.axis_size("dp")
    device = lax.axis_index("dp")
    owners = [matrix_index * (axis_count // 3) for matrix_index in range(3)]
    whole_stack = lax.all_gather(rounded_stack, "dp", axis=1, tiled=True)
    mine = jnp.zeros_like(whole_stack[0])
    for matrix_index in range(3):
        mine = jnp.where(device == owners[matrix_index], whole_stack[matrix_index], mine)
    produced = owner_schulz(mine)
    results = [broadcast(produced, "dp", owner_index) for owner_index in owners]
    ortho = lax.dynamic_slice_in_dim(jnp.stack(results), device * local_rows, local_rows, 1)
    factor = 0.2 * math.sqrt(max(D, INNER))
    muon_new = jnp.stack(
        [gate_weight, inner_weight, output_weight]
    ) - muon_rate * factor * ortho.astype(jnp.float32)
    delta_updated, delta_moment_new = plain_update(delta_weight, delta_moment, delta_sum)
    state_updated, state_moment_new = plain_update(state_weight, state_moment, state_sum)
    filter_updated, filter_moment_new = plain_update(inner_filter, inner_filter_moment, filter_sum)
    state_filter_updated, state_filter_moment_new = plain_update(
        state_filter, state_filter_moment, state_filter_sum
    )
    scalar_updated, scalar_moment_new = plain_update(head_scalars, head_scalars_moment, scalar_sum)
    norm_gain_updated, norm_gain_moment_new = plain_update(
        norm_gain, norm_gain_moment, norm_gain_sum
    )
    input_gain_updated, input_gain_moment_new = plain_update(
        input_gain, input_gain_moment, input_gain_sum
    )
    return (
        block_output,
        input_gradient,
        gate_sum,
        inner_sum,
        output_sum,
        delta_sum,
        state_sum,
        filter_sum,
        state_filter_sum,
        scalar_sum,
        norm_gain_sum,
        input_gain_sum,
        muon_new[0],
        muon_new[1],
        muon_new[2],
        delta_updated,
        state_updated,
        filter_updated,
        state_filter_updated,
        scalar_updated,
        norm_gain_updated,
        input_gain_updated,
        fresh_stack[0],
        fresh_stack[1],
        fresh_stack[2],
        delta_moment_new,
        state_moment_new,
        filter_moment_new,
        state_filter_moment_new,
        scalar_moment_new,
        norm_gain_moment_new,
        input_gain_moment_new,
    )


def solution(mesh):
    placed = (
        P("dp", None),
        P("dp", None),
        P("dp", None),
        P("dp", "tensor"),
        P("dp", "tensor"),
        P("dp", "tensor"),
        P("dp", "tensor"),
        P("dp", None),
        P(None, "tensor"),
        P(),
        P(None, "tensor"),
        P("tensor"),
        P(),
        P("dp", "tensor"),
        P("dp", "tensor"),
        P("dp", "tensor"),
        P("dp", "tensor"),
        P("dp", None),
        P(None, "tensor"),
        P(),
        P(None, "tensor"),
        P("tensor"),
        P(),
    )
    return jax.shard_map(
        local,
        mesh=mesh,
        in_specs=placed,
        out_specs=(
            P("dp", None),
            P("dp", None),
            P("dp", "tensor"),
            P("dp", "tensor"),
            P("dp", "tensor"),
            P("dp", "tensor"),
            P("dp", None),
            P(None, "tensor"),
            P(),
            P(None, "tensor"),
            P("tensor"),
            P(),
            P("dp", "tensor"),
            P("dp", "tensor"),
            P("dp", "tensor"),
            P("dp", "tensor"),
            P("dp", None),
            P(None, "tensor"),
            P(),
            P(None, "tensor"),
            P("tensor"),
            P(),
            P("dp", "tensor"),
            P("dp", "tensor"),
            P("dp", "tensor"),
            P("dp", "tensor"),
            P("dp", None),
            P(None, "tensor"),
            P(),
            P(None, "tensor"),
            P("tensor"),
            P(),
        ),
        check_vma=False,
    )
```

profile of v0, /device:TPU:0, one launch (start us, length us, event | category | flops | bytes accessed | tf_op | source)
XLA Modules:
  0.0 2593.0 jit_solution(2883979421755523016)
XLA Ops:
  20.1 10.8 all-gather
  31.9 12.9 all_gather.21
  44.7 31.0 %all-gather.8.cloned.1.call-done = bf16[1536,768]{1,0:T(8,128)(2,1)} async-done(((bf16[192,768]{1,0:T(8,128)(2,1)}), bf16[1536,768]{1,0:T(8,128)(2,1)}) %all-gather.8.cloned.1.call-update) | async-done | bytes 2359312 | tf_op jit(solution)/shard_map/all_gather | solution.py:174
  75.7 9.7 concatenate.31
  112.6 8.6 while.36
  122.7 7.3 fusion.61
  137.4 12.7 psum.140
  163.2 9.5 psum.142
  192.3 13.0 while.37
  211.3 10.1 fusion.66
  270.7 41.0 %reduce-scatter.16.cloned.1.call-done = f32[192,768]{1,0:T(8,128)} async-done(((f32[1536,768]{1,0:T(8,128)}), f32[192,768]{1,0:T(8,128)}) %reduce-scatter.16.cloned.1.call-update) | async-done | bytes 589840
  313.9 55.4 %reduce-scatter.18.cloned.1.call-done = f32[192,768]{1,0:T(8,128)} async-done(((f32[1536,768]{1,0:T(8,128)}), f32[192,768]{1,0:T(8,128)}) %reduce-scatter.18.cloned.1.call-update) | async-done | bytes 589840
  376.4 48.8 %all-gather.12.cloned.1.call-done = bf16[3,1536,768]{2,1,0:T(8,128)(2,1)} async-done(((bf16[3,192,768]{2,1,0:T(8,128)(2,1)}), bf16[3,1536,768]{2,1,0:T(8,128)(2,1)}) %all-gather.12.cloned.1.call-update) | async-done | bytes 7077904 | tf_op jit(solution)/shard_map/all_gather | solution.py:279
  429.5 12.3 psum.151
  442.5 6.4 fusion.145
  449.0 322.0 %all-reduce.38.cloned.1.call-done = f32[1536,1536]{1,0:T(8,128)} async-done(((f32[1536,1536]{1,0:T(8,128)}), f32[1536,1536]{1,0:T(8,128)}) %all-reduce.38.cloned.1.call-update) | async-done | bytes 9437200 | tf_op jit(solution)/shard_map/psum | solution.py:119
  770.9 22.2 add_convert_fusion.9
  793.2 9.9 fusion.169
  803.5 323.3 %all-reduce.40.cloned.1.call-done = f32[1536,1536]{1,0:T(8,128)} async-done(((f32[1536,1536]{1,0:T(8,128)}), f32[1536,1536]{1,0:T(8,128)}) %all-reduce.40.cloned.1.call-update) | async-done | bytes 9437200 | tf_op jit(solution)/shard_map/psum | solution.py:119
  1126.8 22.2 add_convert_fusion.8
  1149.0 9.9 fusion.170
  1159.1 323.5 %all-reduce.42.cloned.1.call-done = f32[1536,1536]{1,0:T(8,128)} async-done(((f32[1536,1536]{1,0:T(8,128)}), f32[1536,1536]{1,0:T(8,128)}) %all-reduce.42.cloned.1.call-update) | async-done | bytes 9437200 | tf_op jit(solution)/shard_map/psum | solution.py:119
  1482.7 22.8 add_convert_fusion.7
  1505.5 6.4 fusion.171
  1537.2 298.4 %all-reduce.44.cloned.1.call-done = f32[1536,1536]{1,0:T(8,128)} async-done(((f32[1536,1536]{1,0:T(8,128)}), f32[1536,1536]{1,0:T(8,128)}) %all-reduce.44.cloned.1.call-update) | async-done | bytes 9437200 | tf_op jit(solution)/shard_map/psum | solution.py:119
  1835.6 22.6 add_convert_fusion.6
  1866.8 6.3 reduce-scatter.22.cloned.1.call-done
  1874.1 548.8 %all-reduce.46.cloned.1.call-done = (f32[512,1536]{1,0:T(8,128)}, f32[512,1536]{1,0:T(8,128)}, f32[512,256]{0,1:T(8,128)}, f32[1536,1536]{1,0:T(8,128)}) async-done(((f32[512,1536]{1,0:T(8,128)}, f32[512,1536]{1,0:T(8,128)}, f32[512,256]{0,1:T(8,128)}, f32[1536,1536]{1,0:T(8,128)}), (f32[512,1536]{1,0:T(8,128)}, f32[512,1536]{1,0:T(8,128)}, f32[512,256]{0,1:T(8,128)}, ...) | async-done | bytes 16252944 | tf_op jit(solution)/shard_map/psum | solution.py:220
  2429.2 24.8 select_bitcast_fusion.2
  2468.7 26.0 %all-reduce.28 = (f32[5,768]{1,0:T(8,128)S(1)}, f32[5,256]{1,0:T(8,128)S(1)}, f32[3,12]{1,0:T(4,128)S(1)}, f32[768]{0:T(1024)S(1)}, f32[1536]{0:T(1024)S(1)}) all-reduce(f32[5,768]{1,0:T(8,128)S(1)} %pad_add_fusion.1, f32[5,256]{1,0:T(8,128)S(1)} %pad_add_fusion.2, ...), channel_id=1, replica_groups=mesh['dp'=8,'tensor'=4] {'dp'}, use_global_device_ids=true, to_apply=%region_33.34 | all-reduce | flops 7460 | bytes 59680 | tf_op jit(solution)/shard_map/psum | solution.py:268
  2498.0 6.7 fusion.32
  2506.5 76.9 %all-reduce.48.cloned.1.call-done = (bf16[1,1536,768]{2,1,0:T(8,128)(2,1)}, bf16[1,1536,768]{2,1,0:T(8,128)(2,1)}, bf16[1,1536,768]{2,1,0:T(8,128)(2,1)}) async-done(((bf16[1,1536,768]{2,1,0:T(8,128)(2,1)}, bf16[1,1536,768]{2,1,0:T(8,128)(2,1)}, bf16[1,1536,768]{2,1,0:T(8,128)(2,1)}), (bf16[1,1536,768]{2,1,0:T(8,128)(2,1)}, bf16[1,1536,768]{2,1,0:T(8,128)(2,1)}, ...) | async-done | bytes 7077904 | tf_op jit(solution)/shard_map/psum | solution.py:26
  (519 shorter events, 235.2 us)
Async XLA Ops:
  7.3 37.5 %all-gather.6.cloned.1.call-start = ((), (), s32[]{:S(2)}) async-start(), calls=%async_computation.5 | async-start | bytes 2654208 | tf_op jit(solution)/shard_map/all_gather | solution.py:173
  9.3 66.4 %all-gather.8.cloned.1.call-start = ((), (), s32[]{:S(2)}) async-start(), calls=%async_computation.6 | async-start | bytes 2654208 | tf_op jit(solution)/shard_map/all_gather | solution.py:174
  11.2 146.1 %all-gather.10.cloned.1.call-start = ((), (), s32[]{:S(2)}) async-start(), calls=%async_computation.7 | async-start | bytes 2654208 | tf_op jit(solution)/shard_map/all_gather | solution.py:175
  12.0 256.3 %reduce-scatter.20.cloned.1.call-start = ((), (), s32[]{:S(2)}) async-start(), calls=%async_computation.16 | async-start | bytes 5308416
  12.4 96.1 %copy-start.71 = (s32[2,256]{1,0:T(2,128)}, s32[2,256]{1,0:T(2,128)S(1)}, u32[]{:S(2)}) copy-start(s32[2,256]{1,0:T(2,128)S(1)} %eq.65) | copy-start | bytes 6148
  31.9 53.5 %copy-start.44 = (bf16[8,192,12]{2,1,0:T(8,128)(2,1)}, bf16[8,192,12]{2,1,0:T(8,128)(2,1)S(1)}, u32[]{:S(2)}) copy-start(bf16[8,192,12]{2,1,0:T(8,128)(2,1)S(1)} %copy.300) | copy-start | bytes 110596
  44.7 40.6 %copy-start.21 = (bf16[1536,256]{1,0:T(8,128)(2,1)}, bf16[1536,256]{1,0:T(8,128)(2,1)S(1)}, u32[]{:S(2)}) copy-start(bf16[1536,256]{1,0:T(8,128)(2,1)S(1)} %all_gather.21) | copy-start | bytes 2359300
  108.5 102.8 %copy-start.1 = (f32[2,256,12,64]{1,0,3,2:T(2,128)}, f32[2,256,12,64]{1,0,3,2:T(2,128)S(1)}, u32[]{:S(2)}) copy-start(f32[2,256,12,64]{1,0,3,2:T(2,128)S(1)} %reshape.389) | copy-start | bytes 4718596
  181.1 40.7 %copy-start.3 = (f32[2,256,12,64]{1,0,3,2:T(2,128)}, f32[2,256,12,64]{1,0,3,2:T(2,128)S(1)}, u32[]{:S(2)}) copy-start(f32[2,256,12,64]{1,0,3,2:T(2,128)S(1)} %reshape.394) | copy-start | bytes 4718596
  190.7 120.9 %reduce-scatter.16.cloned.1.call-start = ((), (), s32[]{:S(2)}) async-start(), calls=%async_computation.14 | async-start | bytes 5308416
  259.1 110.2 %reduce-scatter.18.cloned.1.call-start = ((), (), s32[]{:S(2)}) async-start(), calls=%async_computation.15 | async-start | bytes 5308416
  265.3 159.9 %all-gather.12.cloned.1.call-start = ((), (), s32[]{:S(2)}) async-start(), calls=%async_computation.9 | async-start | bytes 7962624 | tf_op jit(solution)/shard_map/all_gather | solution.py:279
  376.3 394.6 %all-reduce.38.cloned.1.call-start = ((), (), s32[]{:S(2)}) async-start(), calls=%async_computation.10 | async-start | bytes 18874368 | tf_op jit(solution)/shard_map/psum | solution.py:119
  448.9 677.9 %all-reduce.40.cloned.1.call-start = ((), (), s32[]{:S(2)}) async-start(), calls=%async_computation.11 | async-start | bytes 18874368 | tf_op jit(solution)/shard_map/psum | solution.py:119
  803.0 323.8 %copy-start.154 = (bf16[1536,768]{1,0:T(8,128)(2,1)S(1)}, bf16[1536,768]{1,0:T(8,128)(2,1)}, u32[]{:S(2)}) copy-start(bf16[1536,768]{1,0:T(8,128)(2,1)} %add_convert_fusion.9) | copy-start | bytes 7077892
  803.0 679.6 %all-reduce.42.cloned.1.call-start = ((), (), s32[]{:S(2)}) async-start(), calls=%async_computation.12 | async-start | bytes 18874368 | tf_op jit(solution)/shard_map/psum | solution.py:119
  1158.9 676.7 %all-reduce.44.cloned.1.call-start = ((), (), s32[]{:S(2)}) async-start(), calls=%async_computation.13 | async-start | bytes 18874368 | tf_op jit(solution)/shard_map/psum | solution.py:119
  1511.9 361.3 %reduce-scatter.22.cloned.1.call-start = ((), (), s32[]{:S(2)}) async-start(), calls=%async_computation.17 | async-start | bytes 884736
  1526.9 896.1 %all-reduce.46.cloned.1.call-start = ((), (), s32[]{:S(2)}) async-start(), calls=%async_computation.18 | async-start | bytes 32505856 | tf_op jit(solution)/shard_map/psum | solution.py:220
  1864.6 558.3 %copy-start.28 = (f32[509,256]{0,1:T(8,128)S(1)}, f32[509,256]{0,1:T(8,128)}, u32[]{:S(2)}) copy-start(f32[509,256]{0,1:T(8,128)} %slice.181) | copy-start | bytes 1563652
  1864.6 558.3 %copy-start.43 = (f32[512,256]{0,1:T(8,128)S(1)}, f32[512,256]{0,1:T(8,128)}, u32[]{:S(2)}) copy-start(f32[512,256]{0,1:T(8,128)} %get-tuple-element.585) | copy-start | bytes 1572868
  1864.6 558.3 %copy-start.82 = (f32[512]{0:T(512)S(1)}, f32[512]{0:T(512)}, u32[]{:S(2)}) copy-start(f32[512]{0:T(512)} %get-tuple-element.631) | copy-start | bytes 6148
  1864.7 559.7 %copy-start.25 = (f32[510,256]{0,1:T(8,128)S(1)}, f32[510,256]{0,1:T(8,128)}, u32[]{:S(2)}) copy-start(f32[510,256]{0,1:T(8,128)} %copy-done.24) | copy-start | bytes 1566724
  1864.7 559.7 %copy-start.27 = (f32[511,256]{0,1:T(8,128)S(1)}, f32[511,256]{0,1:T(8,128)}, u32[]{:S(2)}) copy-start(f32[511,256]{0,1:T(8,128)} %copy-done.26) | copy-start | bytes 1569796
  1864.7 559.7 %copy-start.85 = (f32[512]{0:T(512)S(1)}, f32[512]{0:T(512)}, u32[]{:S(2)}) copy-start(f32[512]{0:T(512)} %get-tuple-element.629) | copy-start | bytes 6148
  1864.7 559.7 %copy-start.88 = (f32[512]{0:T(512)S(1)}, f32[512]{0:T(512)}, u32[]{:S(2)}) copy-start(f32[512]{0:T(512)} %get-tuple-element.630) | copy-start | bytes 6148
  1864.7 640.0 %reduce-scatter.14.cloned.1.call-start = ((), (), s32[]{:S(2)}) async-start(), calls=%async_computation.8 | async-start | bytes 1769472 | tf_op jit(solution)/shard_map/reduce_scatter | solution.py:266
  1874.1 579.8 %copy-start.75 = (f32[192,12]{0,1:T(8,128)}, f32[192,12]{0,1:T(8,128)S(1)}, u32[]{:S(2)}) copy-start(f32[192,12]{0,1:T(8,128)S(1)} %copy.299) | copy-start | bytes 27652
  2429.1 154.3 %all-reduce.48.cloned.1.call-start = ((), (), s32[]{:S(2)}) async-start(), calls=%async_computation.19 | async-start | bytes 14155776 | tf_op jit(solution)/shard_map/psum | solution.py:26
  2497.9 85.5 %copy-start.38 = (f32[192,768]{1,0:T(8,128)S(1)}, f32[192,768]{1,0:T(8,128)}, u32[]{:S(2)}) copy-start(f32[192,768]{1,0:T(8,128)} %param.30) | copy-start | bytes 1769476
  2498.0 85.5 %copy-start.39 = (f32[192,768]{1,0:T(8,128)S(1)}, f32[192,768]{1,0:T(8,128)}, u32[]{:S(2)}) copy-start(f32[192,768]{1,0:T(8,128)} %param.31) | copy-start | bytes 1769476
  2498.0 85.4 %copy-start.41 = (f32[192,768]{1,0:T(8,128)S(1)}, f32[192,768]{1,0:T(8,128)}, u32[]{:S(2)}) copy-start(f32[192,768]{1,0:T(8,128)} %param.32) | copy-start | bytes 1769476
  (140 other events, 841.6 us)
Sparse Core Ops, SparseCore 0:
  10.5 33.7 all-gather.5
  46.8 28.8 all-gather.7
  78.2 28.9 all-gather.9
  190.8 52.4 reduce-scatter.19
  259.2 52.3 reduce-scatter.15
  315.5 53.7 reduce-scatter.17
  376.4 48.7 all-gather.11
  449.0 321.8 all-reduce.37
  803.2 323.5 all-reduce.39
  1159.0 323.5 all-reduce.41
  1512.0 323.5 all-reduce.43
  1839.2 33.9 reduce-scatter.21
  1877.2 545.6 all-reduce.45
  2429.2 37.2 reduce-scatter.13
  2470.0 113.3 all-reduce.47
where the time goes:
time: 2600 us; the launch traced here: 2590 us
  waiting for transfers between devices  2080 us (80%)
  matrix products  237 us (9%)
  local copies, waits for them, and re-layouts  93.2 us (4%)
  blocking collectives  84.1 us (3%)
  other arithmetic  83.5 us (3%)
    psum x4, waiting for transfers between devices, tensor_total(): return lax.psum(values, 'tensor')  1270 us
    psum x1, waiting for transfers between devices, local(): lax.psum(partial_out, 'tensor')  549 us
    dot_general x5, matrix products, owner_schulz(): jnp.dot(polynomial, iterate, preferred_element_type=jnp.float32)  115 us
    unnamed x19, waiting for transfers between devices  103 us
    psum x1, waiting for transfers between devices, broadcast(): return lax.psum(block, axis)  76.9 us
  transfers between devices with their start and end apart: 15, of which 11 were waited for; matrix products, arithmetic and copies ran while one was open for 10% of the time, Pallas kernels for 0%

commit v1 on v0

--- a/solution.py
+++ b/solution.py
@@ -3,6 +3,8 @@
 import jax
 import jax.numpy as jnp
 from jax import lax
+from jax.experimental import pallas as pl
+from jax.experimental.pallas import tpu as pltpu
 from jax.sharding import PartitionSpec as P
 
 D = 1536
@@ -11,6 +13,9 @@
 CONV = 4
 SPAN = 256
 SCHULZ = 5
+GROUP = 3
+TILE = 256
+SLAB = 512
 
 
 norm_epsilon = 1e-05
@@ -19,11 +24,6 @@
 plain_rate = 0.002
 schulz_terms = (3.4445, -4.775, 2.0315)
 exact_mode = lax.Precision.HIGHEST
-
-
-def broadcast(block, axis, holder):
-    block = jnp.where(lax.axis_index(axis) == holder, block, jnp.zeros_like(block))
-    return lax.psum(block, axis)
 
 
 def packing_layout(length_row, row_count):
@@ -115,26 +115,235 @@
     return outputs.reshape(row_count, head_count * head_width) * jax.nn.silu(gate_part)
 
 
-def tensor_total(values):
-    return lax.psum(values, "tensor")
-
-
-def owner_schulz(rounded):
-    widened = rounded.astype(jnp.float32)
-    frobenius = jnp.sqrt(tensor_total(jnp.sum(widened * widened)))
-    iterate = (widened / (frobenius + 1e-07)).astype(jnp.bfloat16)
-    for sweep in range(SCHULZ):
-        gram_matrix = tensor_total(jnp.dot(iterate, iterate.T, preferred_element_type=jnp.float32))
-        gram_low = gram_matrix.astype(jnp.bfloat16)
-        squared = jnp.dot(gram_low, gram_low, preferred_element_type=jnp.float32)
-        polynomial = (schulz_terms[1] * gram_matrix + schulz_terms[2] * squared).astype(
-            jnp.bfloat16
+def schulz_kernel(
+    place, pieces, result, iterate, gram, mixed, low, poly, mixed_low, product, arrived
+):
+    holders, column_blocks, rows, columns = pieces.shape
+    width = iterate.shape[0]
+    blocks = width // TILE
+    lead, slope, curve = schulz_terms
+
+    def piece_copy(index):
+        holder = index // column_blocks
+        block = index % column_blocks
+        return pltpu.make_async_copy(
+            pieces.at[holder, block],
+            iterate.at[
+                pl.ds(pl.multiple_of(holder * rows, rows), rows),
+                pl.ds(pl.multiple_of(block * columns, columns), columns),
+            ],
+            arrived.at[index],
         )
-        iterate = (
-            schulz_terms[0] * iterate.astype(jnp.float32)
-            + jnp.dot(polynomial, iterate, preferred_element_type=jnp.float32)
+
+    def begin(index, carry):
+        piece_copy(index).start()
+        return carry
+
+    def finish(index, carry):
+        piece_copy(index).wait()
+        return carry
+
+    lax.fori_loop(0, holders * column_blocks, begin, 0)
+    lax.fori_loop(0, holders * column_blocks, finish, 0)
+    unit_rows = lax.broadcasted_iota(jnp.int32, (TILE, TILE), 0)
+    unit_columns = lax.broadcasted_iota(jnp.int32, (TILE, TILE), 1)
+    diagonal = unit_rows == unit_columns
+    unit = jnp.where(diagonal, 1.0, 0.0).astype(jnp.bfloat16)
+
+    def band(index):
+        return slice(index * TILE, (index + 1) * TILE)
+
+    def tail(index):
+        return slice(index * TILE, width)
+
+    def mirror(target):
+        for upper in range(blocks):
+            for right in range(upper + 1, blocks):
+                flipped = lax.dot_general(
+                    unit,
+                    target[band(upper), band(right)],
+                    (((1,), (1,)), ((), ())),
+                    preferred_element_type=jnp.float32,
+                )
+                target[band(right), band(upper)] = flipped.astype(jnp.bfloat16)
+
+    def half_product(left, right, finish_band):
+        for index in range(blocks):
+            finish_band(
+                index,
+                jnp.dot(
+                    left[band(index), :],
+                    right[:, tail(index)],
+                    preferred_element_type=jnp.float32,
+                ),
+            )
+
+    def sweep(step, carry):
+        lead_power, shrink = carry
+        opening = (step == 0) | (step == GROUP)
+
+        @pl.when(opening)
+        def _():
+            for index in range(blocks):
+                gram[band(index), tail(index)] = lax.dot_general(
+                    iterate[band(index), :],
+                    iterate[tail(index), :],
+                    (((1,), (1,)), ((), ())),
+                    preferred_element_type=jnp.float32,
+                )
+
+        trace = jnp.float32(0.0)
+        for index in range(blocks):
+            trace = trace + jnp.sum(jnp.where(diagonal, gram[band(index), band(index)], 0.0))
+        shrink = jnp.where(
+            step == 0, 1.0 / (jnp.sqrt(jnp.full((1, 1), trace)) + 1e-07), shrink
+        )
+        square = shrink * shrink
+
+        @pl.when(opening)
+        def _():
+            scale = jnp.where(step == 0, square, jnp.ones_like(square))
+            for index in range(blocks):
+                scaled = gram[band(index), tail(index)] * scale
+                gram[band(index), tail(index)] = scaled
+                low[band(index), tail(index)] = scaled.astype(jnp.bfloat16)
+            mirror(low)
+
+        def keep_poly(index, squared):
+            poly[band(index), tail(index)] = (
+                slope * gram[band(index), tail(index)] + curve * squared
+            ).astype(jnp.bfloat16)
+
+        half_product(low, low, keep_poly)
+        mirror(poly)
+        newest = product.at[step % 2]
+        older = product.at[(step + 1) % 2]
+
+        @pl.when(opening)
+        def _():
+            newest[...] = poly[...]
+
+        @pl.when(jnp.logical_not(opening))
+        def _():
+            def keep_product(index, multiplied):
+                newest[band(index), tail(index)] = (
+                    lead * older[band(index), tail(index)].astype(jnp.float32)
+                    + lead_power * poly[band(index), tail(index)].astype(jnp.float32)
+                    + multiplied
+                ).astype(jnp.bfloat16)
+
+            half_product(poly, older, keep_product)
+            mirror(newest)
+
+        lead_power = jnp.where(opening, jnp.float32(lead), lead_power * lead)
+
+        @pl.when(step != GROUP - 1)
+        def _():
+            def keep_mixed(index, multiplied):
+                grown = lead * gram[band(index), tail(index)] + multiplied
+                mixed[band(index), tail(index)] = grown
+                mixed_low[band(index), tail(index)] = grown.astype(jnp.bfloat16)
+
+            half_product(poly, low, keep_mixed)
+
+            @pl.when(step == GROUP)
+            def _():
+                for index in range(blocks):
+                    older[band(index), tail(index)] = (
+                        gram[band(index), tail(index)]
+                        - low[band(index), tail(index)].astype(jnp.float32)
+                    ).astype(jnp.bfloat16)
+                mirror(older)
+
+                def add_rest(index, multiplied):
+                    grown = mixed[band(index), tail(index)] + multiplied
+                    mixed[band(index), tail(index)] = grown
+                    mixed_low[band(index), tail(index)] = grown.astype(jnp.bfloat16)
+
+                half_product(poly, older, add_rest)
+
+            mirror(mixed_low)
+
+            def keep_gram(index, multiplied):
+                fresh = lead * mixed[band(index), tail(index)] + multiplied
+                gram[band(index), tail(index)] = fresh
+                low[band(index), tail(index)] = fresh.astype(jnp.bfloat16)
+
+            half_product(poly, mixed_low, keep_gram)
+            mirror(low)
+
+        @pl.when(step == GROUP - 1)
+        def _():
+            def advance(block, carry):
+                here = pl.ds(pl.multiple_of(block * SLAB, SLAB), SLAB)
+                moved = jnp.dot(newest[...], iterate[:, here], preferred_element_type=jnp.float32)
+                iterate[:, here] = (
+                    shrink * (lead_power * iterate[:, here].astype(jnp.float32) + moved)
+                ).astype(jnp.bfloat16)
+                return carry
+
+            lax.fori_loop(0, iterate.shape[1] // SLAB, advance, 0)
+
+        return lead_power, shrink
+
+    lead_power, shrink = lax.fori_loop(
+        0, SCHULZ - 1, sweep, (jnp.float32(1.0), jnp.ones((1, 1), jnp.float32))
+    )
+    last = product.at[(SCHULZ - 2) % 2]
+    rest = product.at[(SCHULZ - 1) % 2]
+    for index in range(blocks):
+        rest[band(index), tail(index)] = (
+            gram[band(index), tail(index)] - low[band(index), tail(index)].astype(jnp.float32)
         ).astype(jnp.bfloat16)
-    return iterate
+    mirror(rest)
+    mine = pl.ds(pl.multiple_of(place[0] * rows, rows), rows)
+    squared = jnp.dot(low[mine, :], low[...], preferred_element_type=jnp.float32)
+    own_gram = low[mine, :].astype(jnp.float32) + rest[mine, :].astype(jnp.float32)
+    own_poly = (slope * own_gram + curve * squared).astype(jnp.bfloat16)
+    own_product = (
+        lead * last[mine, :].astype(jnp.float32)
+        + lead_power * own_poly.astype(jnp.float32)
+        + jnp.dot(own_poly, last[...], preferred_element_type=jnp.float32)
+    )
+    own_high = own_product.astype(jnp.bfloat16)
+    own_low = (own_product - own_high.astype(jnp.float32)).astype(jnp.bfloat16)
+    for block in range(column_blocks):
+        here = slice(block * columns, (block + 1) * columns)
+        moved = jnp.dot(own_high, iterate[:, here], preferred_element_type=jnp.float32)
+        moved = moved + jnp.dot(own_low, iterate[:, here], preferred_element_type=jnp.float32)
+        result[block] = (
+            (lead_power * lead) * iterate[mine, here].astype(jnp.float32) + moved
+        ).astype(jnp.bfloat16)
+
+
+def own_schulz(pieces, place):
+    holders, column_blocks, rows, columns = pieces.shape
+    width = holders * rows
+    flops = 2 * width * width * (10 * width + 3 * column_blocks * columns)
+    return pl.pallas_call(
+        schulz_kernel,
+        name="schulz",
+        out_shape=jax.ShapeDtypeStruct((column_blocks, rows, columns), jnp.bfloat16),
+        in_specs=[
+            pl.BlockSpec(memory_space=pltpu.SMEM),
+            pl.BlockSpec(memory_space=pl.ANY),
+        ],
+        out_specs=pl.BlockSpec(memory_space=pltpu.VMEM),
+        scratch_shapes=[
+            pltpu.VMEM((width, column_blocks * columns), jnp.bfloat16),
+            pltpu.VMEM((width, width), jnp.float32),
+            pltpu.VMEM((width, width), jnp.float32),
+            pltpu.VMEM((width, width), jnp.bfloat16),
+            pltpu.VMEM((width, width), jnp.bfloat16),
+            pltpu.VMEM((width, width), jnp.bfloat16),
+            pltpu.VMEM((2, width, width), jnp.bfloat16),
+            pltpu.SemaphoreType.DMA((holders * column_blocks,)),
+        ],
+        compiler_params=pltpu.CompilerParams(vmem_limit_bytes=62 * 1024 * 1024),
+        cost_estimate=pl.CostEstimate(
+            flops=flops, bytes_accessed=4 * width * columns * column_blocks, transcendentals=0
+        ),
+    )(place, pieces)
 
 
 def plain_update(weight, moment, gradient):
@@ -254,35 +463,29 @@
         + root_scale * weighted_in
         - tokens_wide * root_scale**3 * row_mean
     )
-    gate_sum, inner_sum, output_sum, delta_sum, state_sum = (
-        lax.psum_scatter(mixing_weight_grad[:, :columns], "dp", scatter_dimension=0, tiled=True),
-        lax.psum_scatter(
-            mixing_weight_grad[:, columns : 2 * columns], "dp", scatter_dimension=0, tiled=True
-        ),
-        lax.psum_scatter(output_local, "dp", scatter_dimension=0, tiled=True),
-        lax.psum_scatter(
-            mixing_weight_grad[:, 2 * columns :], "dp", scatter_dimension=0, tiled=True
-        ),
-        lax.psum_scatter(state_local, "dp", scatter_dimension=0, tiled=True),
-    )
+    def scattered(partial):
+        low = partial.astype(jnp.bfloat16)
+        return lax.psum_scatter(low, "dp", scatter_dimension=0, tiled=True).astype(jnp.float32)
+
+    output_sum = scattered(output_local)
+    gate_sum = scattered(mixing_weight_grad[:, :columns])
+    inner_sum = scattered(mixing_weight_grad[:, columns : 2 * columns])
+    delta_sum = lax.psum_scatter(
+        mixing_weight_grad[:, 2 * columns :], "dp", scatter_dimension=0, tiled=True
+    )
+    state_sum = lax.psum_scatter(state_local, "dp", scatter_dimension=0, tiled=True)
     filter_sum, state_filter_sum, scalar_sum, norm_gain_sum, input_gain_sum = lax.psum(
         (filter_local, state_filter_local, scalar_local, norm_gain_local, input_gain_local), "dp"
     )
     fresh_stack = moment_decay * jnp.stack([gate_moment, inner_moment, output_moment]) + jnp.stack(
         [gate_sum, inner_sum, output_sum]
     )
-    rounded_stack = fresh_stack.astype(jnp.bfloat16)
-    local_rows = rounded_stack.shape[1]
-    axis_count = lax.axis_size("dp")
-    device = lax.axis_index("dp")
-    owners = [matrix_index * (axis_count // 3) for matrix_index in range(3)]
-    whole_stack = lax.all_gather(rounded_stack, "dp", axis=1, tiled=True)
-    mine = jnp.zeros_like(whole_stack[0])
-    for matrix_index in range(3):
-        mine = jnp.where(device == owners[matrix_index], whole_stack[matrix_index], mine)
-    produced = owner_schulz(mine)
-    results = [broadcast(produced, "dp", owner_index) for owner_index in owners]
-    ortho = lax.dynamic_slice_in_dim(jnp.stack(results), device * local_rows, local_rows, 1)
+    spare = jnp.zeros((lax.axis_size("tensor") - 3,) + fresh_stack.shape[1:], jnp.bfloat16)
+    rounded_stack = jnp.concatenate([fresh_stack.astype(jnp.bfloat16), spare], axis=0)
+    own_rows = lax.all_to_all(rounded_stack, "tensor", split_axis=0, concat_axis=0, tiled=True)
+    whole = lax.all_gather(own_rows, "dp", axis=0)
+    produced = own_schulz(whole, lax.axis_index("dp").reshape(1).astype(jnp.int32))
+    ortho = lax.all_to_all(produced, "tensor", split_axis=0, concat_axis=0, tiled=True)[:3]
     factor = 0.2 * math.sqrt(max(D, INNER))
     muon_new = jnp.stack(
         [gate_weight, inner_weight, output_weight]

time: 2600 us -> 924 us (0.36)
  waiting for transfers between devices: 2080 us -> 376 us
  matrix products: 237 us -> 90.6 us
  Pallas kernels: 0 us -> 143 us
    psum x5 -> x0, waiting for transfers between devices: 1340 us -> none  [the longest x4 1270 us: tensor_total(): return lax.psum(values, 'tensor')]
    psum x1, waiting for transfers between devices: 549 us -> 227 us  [local(): lax.psum(partial_out, 'tensor')]
    dot_general x10 -> x0, matrix products: 153 us -> none  [the longest x5 115 us: owner_schulz(): jnp.dot(polynomial, iterate, preferred_element_type=jnp.float32)]
    pallas_call x0 -> x1, Pallas kernels: none -> 143 us  [own_schulz(): pl.pallas_call(schulz_kernel, name='schulz', out_shape=jax.ShapeDtypeStru...]
    all_to_all x0 -> x1, blocking collectives: none -> 33 us  [local(): lax.all_to_all(rounded_stack, 'tensor', split_axis=0, concat_axis=0, tile...]
    all_gather x1, waiting for transfers between devices: 48.8 us -> 20.3 us  [local(): whole = lax.all_gather(own_rows, 'dp', axis=0)]
    unnamed x19 -> x14, waiting for transfers between devices: 103 us -> 82.7 us
  transfers between devices with their start and end apart: 15 -> 11, of which waited for: 11 -> 6; matrix products, arithmetic and copies ran while one was open for 10% -> 19% of each run, Pallas kernels for 0% -> 16%
where the time goes in v1:
time: 924 us; the launch traced here: 919 us
  waiting for transfers between devices  376 us (41%)
  Pallas kernels  143 us (15%)
  blocking collectives  103 us (11%)
  local copies, waits for them, and re-layouts  101 us (11%)
  matrix products  90.6 us (10%)
  other arithmetic  84 us (9%)
  between operations  16.2 us (2%)
    psum x1, waiting for transfers between devices, local(): lax.psum(partial_out, 'tensor')  227 us
    pallas_call x1, Pallas kernels, own_schulz(): pl.pallas_call(schulz_kernel, name='schulz', out_shape=jax.ShapeDtypeStru...  143 us
    unnamed x14, waiting for transfers between devices  82.7 us
    unnamed x335, local copies, waits for them, and re-layouts  42.3 us
    all_to_all x1, blocking collectives, local(): lax.all_to_all(rounded_stack, 'tensor', split_axis=0, concat_axis=0, tile...  33 us
    all_gather x1, waiting for transfers between devices, local(): lax.all_gather(inner_weight.astype(jnp.bfloat16), 'dp', axis=0, tiled=True)  26.8 us
    psum x1, blocking collectives, local(): lax.psum((filter_local, state_filter_local, scalar_local, norm_gain_local...  25.6 us
    dot_general x3, matrix products, state_mixer(): within = jnp.einsum('cijh,cjhp->cihp', mixing, driven, precision=exact_mode)  23.3 us
  transfers between devices with their start and end apart: 11, of which 6 were waited for; matrix products, arithmetic and copies ran while one was open for 19% of the time, Pallas kernels for 16%

profile of v1, /device:TPU:0, one launch (start us, length us, event | category | flops | bytes accessed | tf_op | source)
XLA Modules:
  0.0 918.8 jit_solution(8014470330726837044)
XLA Ops:
  14.8 10.7 %all-gather.1 = bf16[8,192,12]{1,2,0:T(8,128)(2,1)S(1)} all-gather(bf16[1,192,12]{1,2,0:T(8,128)(2,1)S(1)} %convert_bitcast_fusion.3), channel_id=1, replica_groups=mesh['dp'=8,'tensor'=4] {'dp'}, dimensions={0}, use_global_device_ids=true | all-gather | bytes 41472 | tf_op jit(solution)/shard_map/all_gather | solution.py:385
  25.9 12.4 %all_gather.24 = bf16[1536,256]{1,0:T(8,128)(2,1)S(1)} all-gather(bf16[192,256]{1,0:T(8,128)(2,1)S(1)} %convert_element_type.114), channel_id=1, replica_groups=mesh['dp'=8,'tensor'=4] {'dp'}, dimensions={0}, use_global_device_ids=true | all-gather | bytes 884736 | tf_op jit(solution)/shard_map/all_gather | solution.py:386
  47.8 26.8 %all-gather.9.cloned.1.call-done = bf16[1536,768]{1,0:T(8,128)(2,1)} async-done(((bf16[192,768]{1,0:T(8,128)(2,1)}), bf16[1536,768]{1,0:T(8,128)(2,1)}) %all-gather.9.cloned.1.call-update) | async-done | bytes 2359312 | tf_op jit(solution)/shard_map/all_gather | solution.py:383
  74.6 9.8 %concatenate.34 = bf16[1536,1804]{1,0:T(8,128)(2,1)} concatenate(bf16[1536,768]{1,0:T(8,128)(2,1)} %all-gather.7.cloned.1.call-done, bf16[1536,768]{1,0:T(8,128)(2,1)} %all-gather.9.cloned.1.call-done, bf16[1536,12]{1,0:T(8,128)(2,1)S(1)} %bitcast.238, bf16[1536,256]{1,0:T(8,128)(2,1)S(1)} %all_gather.24), dimensions={1} | concatenate | bytes 11083776 | tf_op jit(solution)/shard_map/concatenate | solution.py:391
  84.4 6.1 fusion.137
  99.3 4.7 fusion.55
  117.7 10.5 %while.36 = (s32[]{:T(128)}, f32[12,64,128]{2,1,0:T(8,128)S(1)}, f32[2,12,64,128]{3,2,1,0:T(8,128)}, f32[2,12]{1,0:T(2,128)}, f32[2,12,1,1]{1,3,2,0:T(1,128)}, /...) while((s32[]{:T(128)}, f32[12,64,128]{2,1,0:T(8,128)S(1)}, ...), condition=%wide.region_5.6_spmd.clone, body=%wide.region_4.5_spmd.clone.sunk | while | flops 393243 | bytes 1968056 | solution.py:105
  131.0 7.6 fusion.52
  145.9 12.4 %psum.77 = f32[512]{0:T(512)} all-reduce(f32[512]{0:T(512)} %get-tuple-element.574), channel_id=1, replica_groups=mesh['dp'=8,'tensor'=4] {'tensor'}, use_global_device_ids=true, to_apply=%region_7.8 | all-reduce | flops 512 | bytes 4096 | tf_op jit(solution)/shard_map/psum | solution.py:423
  159.5 5.9 multiply_reduce_fusion.1
  165.5 9.2 %psum.79 = f32[512]{0:T(512)} all-reduce(f32[512]{0:T(512)} %get-tuple-element.484), channel_id=1, replica_groups=mesh['dp'=8,'tensor'=4] {'tensor'}, use_global_device_ids=true, to_apply=%region_10.11 | all-reduce | flops 512 | bytes 4096 | tf_op jit(solution)/shard_map/psum | solution.py:436
  175.4 5.8 multiply_reduce_fusion.2
  188.2 10.1 %fusion.57 = (f32[2,256,12]{1,2,0:T(8,128)}, f32[2,256,12]{1,2,0:T(8,128)}, f32[2,256,256]{2,1,0:T(8,128)}) fusion(f32[2,256,12]{1,2,0:T(8,128)S(1)} %copy-done.70, f32[2,256,256]{2,1,0:T(8,128)S(1)} %copy-done.66, f32[2,256,12,64]{1,0,3,2:T(2,128)S(1)} %copy-done.2, f32[2,256,12]{1,2,0:T(8,128)S(1)} %copy-done.61, f32[2,256,12,64]{1,0,3,2:T(2,128)S(1)} %copy-done.3), kind=kOutput, calls=%fused_computation.107 | convolution fusion | flops 1228656640 | bytes 4292608 | tf_op jit(solution)/shard_map/transpose(jvp(cijh,cjhp->cihp))/dot_general | solution.py:84
  200.8 13.1 %while.37 = (s32[]{:T(128)}, f32[12,64,128]{2,1,0:T(8,128)S(1)}, f32[2,12]{1,0:T(2,128)}, f32[2,12,64,128]{3,2,1,0:T(8,128)}, f32[2,12,64,128]{3,2,1,0:T(8,128)}...) while((s32[]{:T(128)}, f32[12,64,128]{2,1,0:T(8,128)S(1)}, ...), condition=%wide.region_13.14_spmd.clone, body=%wide.region_11.13_spmd.clone.sunk | while | flops 589840 | bytes 2359964 | solution.py:105
  216.8 5.5 bitcast_add_fusion.2
  244.2 7.4 fusion.151
  258.4 4.3 copy.264
  263.4 4.9 fusion.37
  268.4 4.7 copy.266
  291.0 5.1 fusion.133
  296.2 4.8 fusion.14
  307.5 38.0 %reduce-scatter.18.cloned.1.call-done = bf16[192,768]{1,0:T(8,128)(2,1)} async-done(((bf16[1536,768]{1,0:T(8,128)(2,1)}), bf16[192,768]{1,0:T(8,128)(2,1)}) %reduce-scatter.18.cloned.1.call-update) | async-done | bytes 294928
  346.7 44.5 %reduce-scatter.20.cloned.1.call-done = bf16[192,768]{1,0:T(8,128)(2,1)} async-done(((bf16[1536,768]{1,0:T(8,128)(2,1)}), bf16[192,768]{1,0:T(8,128)(2,1)}) %reduce-scatter.20.cloned.1.call-update) | async-done | bytes 294928
  398.6 33.0 %all_to_all.10 = bf16[4,192,768]{2,1,0:T(8,128)(2,1)} all-to-all(bf16[4,192,768]{2,1,0:T(8,128)(2,1)S(1)} %concatenate.44.clone), channel_id=1, replica_groups=mesh['dp'=8,'tensor'=4] {'tensor'}, dimensions={0} | all-to-all | bytes 2359296 | tf_op jit(solution)/shard_map/all_to_all | solution.py:485
  446.1 226.7 %all-reduce.33.cloned.1.call-done = (f32[512,1536]{1,0:T(8,128)}, f32[512,1536]{1,0:T(8,128)}, f32[512,256]{0,1:T(8,128)}) async-done(((f32[512,1536]{1,0:T(8,128)}, f32[512,1536]{1,0:T(8,128)}, f32[512,256]{0,1:T(8,128)}), (f32[512,1536]{1,0:T(8,128)}, f32[512,1536]{1,0:T(8,128)}, f32[512,256]{0,1:T(8,128)})) %all-reduce.33.cloned.1.call-update) | async-done | bytes 6815760 | tf_op jit(solution)/shard_map/psum | solution.py:429
  679.2 5.1 fusion.28
  685.0 25.6 %all-reduce.29 = (f32[5,768]{1,0:T(8,128)S(1)}, f32[5,256]{1,0:T(8,128)S(1)}, f32[3,12]{1,0:T(4,128)S(1)}, f32[768]{0:T(1024)S(1)}, f32[1536]{0:T(1024)S(1)}) all-reduce(f32[5,768]{1,0:T(8,128)S(1)} %copy-done.78, f32[5,256]{1,0:T(8,128)S(1)} %pad_add_fusion.2, ...), channel_id=1, replica_groups=mesh['dp'=8,'tensor'=4] {'dp'}, use_global_device_ids=true, to_apply=%region_33.34 | all-reduce | flops 7460 | bytes 59680 | tf_op jit(solution)/shard_map/psum | solution.py:477
  712.5 20.3 %all-gather.13.cloned.1.call-done = bf16[32,192,768]{2,1,0:T(8,128)(2,1)} async-done(((bf16[4,192,768]{2,1,0:T(8,128)(2,1)}), bf16[32,192,768]{2,1,0:T(8,128)(2,1)}) %all-gather.13.cloned.1.call-update) | async-done | bytes 9437200 | tf_op jit(solution)/shard_map/all_gather | solution.py:486
  732.8 142.7 %schulz.1 = bf16[4,192,768]{2,1,0:T(8,128)(2,1)} custom-call(s32[1]{0:T(128)} %bitcast.49.place, bf16[8,4,192,768]{3,2,1,0:T(8,128)(2,1)} %bitcast.264), custom_call_target="tpu_custom_call" | custom-call | flops 115964116992 | bytes 18874368 | tf_op jit(solution)/shard_map/schulz/pallas_call | solution.py:323
  875.6 4.5 all-to-all-start.1
  881.4 6.6 fusion.25
  889.9 19.2 %all-to-all-done.1 = bf16[4,192,768]{2,1,0:T(8,128)(2,1)S(1)} async-done(((bf16[4,192,768]{2,1,0:T(8,128)(2,1)}), bf16[4,192,768]{2,1,0:T(8,128)(2,1)S(1)}, u32[]{:S(2)}, u32[]{:S(2)}) %all-to-all-start.1) | async-done | bytes 1179680 | tf_op jit(solution)/shard_map/all_to_all | solution.py:488
  (506 shorter events, 177.9 us)
Async XLA Ops:
  7.2 40.6 %all-gather.7.cloned.1.call-start = ((), (), s32[]{:S(2)}) async-start(), calls=%async_computation.7 | async-start | bytes 2654208 | tf_op jit(solution)/shard_map/all_gather | solution.py:382
  9.2 65.4 %all-gather.9.cloned.1.call-start = ((), (), s32[]{:S(2)}) async-start(), calls=%async_computation.8 | async-start | bytes 2654208 | tf_op jit(solution)/shard_map/all_gather | solution.py:383
  10.0 149.5 %all-gather.11.cloned.1.call-start = ((), (), s32[]{:S(2)}) async-start(), calls=%async_computation.9 | async-start | bytes 2654208 | tf_op jit(solution)/shard_map/all_gather | solution.py:384
  10.9 295.5 %reduce-scatter.16.cloned.1.call-start = ((), (), s32[]{:S(2)}) async-start(), calls=%async_computation.12 | async-start | bytes 2654208
  25.8 58.6 %copy-start.50 = (bf16[8,192,12]{2,1,0:T(8,128)(2,1)}, bf16[8,192,12]{2,1,0:T(8,128)(2,1)S(1)}, u32[]{:S(2)}) copy-start(bf16[8,192,12]{2,1,0:T(8,128)(2,1)S(1)} %copy.270) | copy-start | bytes 110596
  38.3 46.2 %copy-start.15 = (bf16[1536,256]{1,0:T(8,128)(2,1)}, bf16[1536,256]{1,0:T(8,128)(2,1)S(1)}, u32[]{:S(2)}) copy-start(bf16[1536,256]{1,0:T(8,128)(2,1)S(1)} %all_gather.24) | copy-start | bytes 2359300
  258.4 87.2 %reduce-scatter.18.cloned.1.call-start = ((), (), s32[]{:S(2)}) async-start(), calls=%async_computation.13 | async-start | bytes 2654208
  262.8 128.4 %reduce-scatter.20.cloned.1.call-start = ((), (), s32[]{:S(2)}) async-start(), calls=%async_computation.14 | async-start | bytes 2654208
  273.1 160.8 %reduce-scatter.22.cloned.1.call-start = ((), (), s32[]{:S(2)}) async-start(), calls=%async_computation.15 | async-start | bytes 884736
  290.8 382.0 %all-reduce.33.cloned.1.call-start = ((), (), s32[]{:S(2)}) async-start(), calls=%async_computation.16 | async-start | bytes 13631488 | tf_op jit(solution)/shard_map/psum | solution.py:429
  301.9 430.9 %all-gather.13.cloned.1.call-start = ((), (), s32[]{:S(2)}) async-start(), calls=%async_computation.11 | async-start | bytes 10616832 | tf_op jit(solution)/shard_map/all_gather | solution.py:486
  398.5 33.2 %copy-start.121 = (f32[768]{0:T(1024)S(1)}, f32[768]{0:T(1024)}, u32[]{:S(2)}) copy-start(f32[768]{0:T(1024)} %get-tuple-element.596) | copy-start | bytes 9220
  398.5 33.2 %copy-start.120 = (f32[768]{0:T(1024)S(1)}, f32[768]{0:T(1024)}, u32[]{:S(2)}) copy-start(f32[768]{0:T(1024)} %get-tuple-element.570) | copy-start | bytes 9220
  398.5 33.3 %copy-start.119 = (f32[768]{0:T(1024)S(1)}, f32[768]{0:T(1024)}, u32[]{:S(2)}) copy-start(f32[768]{0:T(1024)} %get-tuple-element.567) | copy-start | bytes 9220
  398.5 33.3 %copy-start.117 = (f32[768]{0:T(1024)S(1)}, f32[768]{0:T(1024)}, u32[]{:S(2)}) copy-start(f32[768]{0:T(1024)} %get-tuple-element.556) | copy-start | bytes 9220
  398.6 33.5 %copy-start.153 = (f32[12]{0:T(128)S(1)}, f32[12]{0:T(128)}, u32[]{:S(2)}) copy-start(f32[12]{0:T(128)} %get-tuple-element.603) | copy-start | bytes 148
  398.6 34.1 %copy-start.149 = (f32[12]{0:T(128)S(1)}, f32[12]{0:T(128)}, u32[]{:S(2)}) copy-start(f32[12]{0:T(128)} %get-tuple-element.558) | copy-start | bytes 148
  398.6 36.3 %copy-start.83 = (f32[192,12]{0,1:T(8,128)S(1)}, f32[192,12]{0,1:T(8,128)}, u32[]{:S(2)}) copy-start(f32[192,12]{0,1:T(8,128)} %param.33) | copy-start | bytes 27652
  398.6 36.3 %copy-start.124 = (f32[192,12]{0,1:T(8,128)S(1)}, f32[192,12]{0,1:T(8,128)}, u32[]{:S(2)}) copy-start(f32[192,12]{0,1:T(8,128)} %param.43) | copy-start | bytes 27652
  431.6 456.4 %reduce-scatter.14.cloned.1.call-start = ((), (), s32[]{:S(2)}) async-start(), calls=%async_computation.10 | async-start | bytes 1769472 | tf_op jit(solution)/shard_map/reduce_scatter | solution.py:476
  442.8 230.1 %copy-start.25 = (f32[509,256]{0,1:T(8,128)S(1)}, f32[509,256]{0,1:T(8,128)}, u32[]{:S(2)}) copy-start(f32[509,256]{0,1:T(8,128)} %slice.175) | copy-start | bytes 1563652
  442.8 230.1 %copy-start.89 = (f32[512]{0:T(512)S(1)}, f32[512]{0:T(512)}, u32[]{:S(2)}) copy-start(f32[512]{0:T(512)} %get-tuple-element.622) | copy-start | bytes 6148
  446.1 228.3 %copy-start.22 = (f32[510,256]{0,1:T(8,128)S(1)}, f32[510,256]{0,1:T(8,128)}, u32[]{:S(2)}) copy-start(f32[510,256]{0,1:T(8,128)} %copy-done.21) | copy-start | bytes 1566724
  446.1 228.3 %copy-start.24 = (f32[511,256]{0,1:T(8,128)S(1)}, f32[511,256]{0,1:T(8,128)}, u32[]{:S(2)}) copy-start(f32[511,256]{0,1:T(8,128)} %copy-done.23) | copy-start | bytes 1569796
  446.1 228.3 %copy-start.92 = (f32[512]{0:T(512)S(1)}, f32[512]{0:T(512)}, u32[]{:S(2)}) copy-start(f32[512]{0:T(512)} %get-tuple-element.620) | copy-start | bytes 6148
  446.1 228.4 %copy-start.95 = (f32[512]{0:T(512)S(1)}, f32[512]{0:T(512)}, u32[]{:S(2)}) copy-start(f32[512]{0:T(512)} %get-tuple-element.621) | copy-start | bytes 6148
  710.6 164.9 %copy-start.135 = (f32[5,256]{1,0:T(8,128)}, f32[5,256]{1,0:T(8,128)S(1)}, u32[]{:S(2)}) copy-start(f32[5,256]{1,0:T(8,128)S(1)} %get-tuple-element.531) | copy-start | bytes 15364
  710.6 164.9 %copy-start.148 = (f32[768]{0:T(1024)}, f32[768]{0:T(1024)S(1)}, u32[]{:S(2)}) copy-start(f32[768]{0:T(1024)S(1)} %get-tuple-element.533) | copy-start | bytes 9220
  710.6 164.9 %copy-start.151 = (f32[3,12]{1,0:T(4,128)}, f32[3,12]{1,0:T(4,128)S(1)}, u32[]{:S(2)}) copy-start(f32[3,12]{1,0:T(4,128)S(1)} %get-tuple-element.532) | copy-start | bytes 436
  710.7 169.5 %copy-start.136 = (f32[1536]{0:T(1024)}, f32[1536]{0:T(1024)S(1)}, u32[]{:S(2)}) copy-start(f32[1536]{0:T(1024)S(1)} %get-tuple-element.534) | copy-start | bytes 18436
  710.7 170.1 %copy-start.109 = (f32[5,768]{1,0:T(8,128)}, f32[5,768]{1,0:T(8,128)S(1)}, u32[]{:S(2)}) copy-start(f32[5,768]{1,0:T(8,128)S(1)} %get-tuple-element.530) | copy-start | bytes 46084
  875.6 33.5 %all-to-all-start.1 = ((bf16[4,192,768]{2,1,0:T(8,128)(2,1)}), bf16[4,192,768]{2,1,0:T(8,128)(2,1)S(1)}, u32[]{:S(2)}, u32[]{:S(2)}) async-start(bf16[4,192,768]{2,1,0:T(8,128)(2,1)} %schulz.1), calls=%async_computation.2 | async-start | bytes 2359296 | tf_op jit(solution)/shard_map/all_to_all | solution.py:488
  (137 other events, 717.5 us)
Sparse Core Ops, SparseCore 0:
  10.5 32.7 all-gather.6
  45.7 28.8 all-gather.8
  77.1 28.8 all-gather.10
  258.5 41.4 reduce-scatter.15
  303.1 42.3 reduce-scatter.17
  348.8 42.3 reduce-scatter.19
  394.3 34.9 reduce-scatter.21
  433.0 239.8 all-reduce.32
  674.8 57.9 all-gather.12
  736.5 38.3 reduce-scatter.13

commit v2 on v1

--- a/solution.py
+++ b/solution.py
@@ -307,12 +307,13 @@
     )
     own_high = own_product.astype(jnp.bfloat16)
     own_low = (own_product - own_high.astype(jnp.float32)).astype(jnp.bfloat16)
+    halves = jnp.concatenate([own_high, own_low], axis=0)
     for block in range(column_blocks):
         here = slice(block * columns, (block + 1) * columns)
-        moved = jnp.dot(own_high, iterate[:, here], preferred_element_type=jnp.float32)
-        moved = moved + jnp.dot(own_low, iterate[:, here], preferred_element_type=jnp.float32)
+        moved = jnp.dot(halves, iterate[:, here], preferred_element_type=jnp.float32)
         result[block] = (
-            (lead_power * lead) * iterate[mine, here].astype(jnp.float32) + moved
+            (lead_power * lead) * iterate[mine, here].astype(jnp.float32)
+            + (moved[:rows] + moved[rows:])
         ).astype(jnp.bfloat16)
 
 
@@ -420,20 +421,20 @@
         inner_filter,
         head_scalars,
     )
-    squares = lax.psum(jnp.sum(gated * gated, axis=1), "tensor")
+    grad_normalized = jnp.dot(cotangent, full_output, preferred_element_type=jnp.float32)
+    weighted = grad_normalized * norm_gain
+    squares, inner_dot = lax.psum(
+        jnp.stack([jnp.sum(gated * gated, axis=1), jnp.sum(weighted * gated, axis=1)]), "tensor"
+    )
     norm_scale = lax.rsqrt(squares / INNER + norm_epsilon)[:, None]
     normalized = (gated * norm_scale * norm_gain).astype(jnp.bfloat16)
     partial_out = jnp.einsum(
         "ti,di->td", normalized, full_output, preferred_element_type=jnp.float32
     )
-    block_output = (tokens_wide + lax.psum(partial_out, "tensor")).astype(jnp.bfloat16)
-    grad_normalized = jnp.dot(cotangent, full_output, preferred_element_type=jnp.float32)
     output_local = jnp.einsum(
         "td,ti->di", cotangent, normalized, preferred_element_type=jnp.float32
     )
     norm_gain_local = jnp.sum(grad_normalized * gated * norm_scale, axis=0)
-    weighted = grad_normalized * norm_gain
-    inner_dot = lax.psum(jnp.sum(weighted * gated, axis=1), "tensor")
     grad_gated = norm_scale * weighted - gated * norm_scale**3 * (inner_dot / INNER)[:, None]
     grad_gate, grad_inner, grad_delta, grad_entry, grad_readout, filter_local, scalar_local = (
         mixer_back(grad_gated)
@@ -454,8 +455,60 @@
     state_input = jnp.einsum(
         "tk,dk->td", grad_state_low, full_state, preferred_element_type=jnp.float32
     )
-    grad_normed = lax.psum(input_partial, "tensor") + state_input
-    input_gain_local = jnp.sum(grad_normed * tokens_wide * root_scale, axis=0)
+    input_gain_local = jnp.sum(
+        (input_partial + state_input / lax.axis_size("tensor")) * tokens_wide * root_scale, axis=0
+    )
+
+    def scattered(partial):
+        low = partial.astype(jnp.bfloat16)
+        return lax.psum_scatter(low, "dp", scatter_dimension=0, tiled=True).astype(jnp.float32)
+
+    output_sum = scattered(output_local)
+    gate_sum = scattered(mixing_weight_grad[:, :columns])
+    inner_sum = scattered(mixing_weight_grad[:, columns : 2 * columns])
+    filter_sum, state_filter_sum, scalar_sum, norm_gain_sum = lax.psum(
+        (filter_local, state_filter_local, scalar_local, norm_gain_local), "dp"
+    )
+    input_gain_sum = lax.psum(input_gain_local, ("dp", "tensor"))
+    fresh_stack = moment_decay * jnp.stack([gate_moment, inner_moment, output_moment]) + jnp.stack(
+        [gate_sum, inner_sum, output_sum]
+    )
+    spare = jnp.zeros((lax.axis_size("tensor") - 3,) + fresh_stack.shape[1:], jnp.bfloat16)
+    rounded_stack = jnp.concatenate([fresh_stack.astype(jnp.bfloat16), spare], axis=0)
+    (
+        rounded_stack,
+        filter_sum,
+        state_filter_sum,
+        scalar_sum,
+        norm_gain_sum,
+        input_gain_sum,
+    ) = lax.optimization_barrier(
+        (
+            rounded_stack,
+            filter_sum,
+            state_filter_sum,
+            scalar_sum,
+            norm_gain_sum,
+            input_gain_sum,
+        )
+    )
+    own_rows = lax.all_to_all(rounded_stack, "tensor", split_axis=0, concat_axis=0, tiled=True)
+    whole = lax.all_gather(own_rows, "dp", axis=0)
+    side = jnp.concatenate([state_local, mixing_weight_grad[:, 2 * columns :]], axis=1)
+    whole, out_low, input_low, side = lax.optimization_barrier(
+        (whole, partial_out.astype(jnp.bfloat16), input_partial.astype(jnp.bfloat16), side)
+    )
+    out_total, input_total = lax.psum((out_low, input_low), "tensor")
+    side_sum = lax.psum_scatter(side, "dp", scatter_dimension=0, tiled=True)
+    produced = own_schulz(whole, lax.axis_index("dp").reshape(1).astype(jnp.int32))
+    out_total, input_total, side_sum, _ = lax.optimization_barrier(
+        (out_total, input_total, side_sum, produced[0, :16, :128])
+    )
+    ortho = lax.all_to_all(produced, "tensor", split_axis=0, concat_axis=0, tiled=True)[:3]
+    state_sum = side_sum[:, : 2 * NSTATE]
+    delta_sum = side_sum[:, 2 * NSTATE :]
+    block_output = (tokens_wide + out_total.astype(jnp.float32)).astype(jnp.bfloat16)
+    grad_normed = input_total.astype(jnp.float32) + state_input
     weighted_in = grad_normed * input_gain
     row_mean = jnp.mean(weighted_in * tokens_wide, axis=1, keepdims=True)
     input_gradient = (
@@ -463,29 +516,6 @@
         + root_scale * weighted_in
         - tokens_wide * root_scale**3 * row_mean
     )
-    def scattered(partial):
-        low = partial.astype(jnp.bfloat16)
-        return lax.psum_scatter(low, "dp", scatter_dimension=0, tiled=True).astype(jnp.float32)
-
-    output_sum = scattered(output_local)
-    gate_sum = scattered(mixing_weight_grad[:, :columns])
-    inner_sum = scattered(mixing_weight_grad[:, columns : 2 * columns])
-    delta_sum = lax.psum_scatter(
-        mixing_weight_grad[:, 2 * columns :], "dp", scatter_dimension=0, tiled=True
-    )
-    state_sum = lax.psum_scatter(state_local, "dp", scatter_dimension=0, tiled=True)
-    filter_sum, state_filter_sum, scalar_sum, norm_gain_sum, input_gain_sum = lax.psum(
-        (filter_local, state_filter_local, scalar_local, norm_gain_local, input_gain_local), "dp"
-    )
-    fresh_stack = moment_decay * jnp.stack([gate_moment, inner_moment, output_moment]) + jnp.stack(
-        [gate_sum, inner_sum, output_sum]
-    )
-    spare = jnp.zeros((lax.axis_size("tensor") - 3,) + fresh_stack.shape[1:], jnp.bfloat16)
-    rounded_stack = jnp.concatenate([fresh_stack.astype(jnp.bfloat16), spare], axis=0)
-    own_rows = lax.all_to_all(rounded_stack, "tensor", split_axis=0, concat_axis=0, tiled=True)
-    whole = lax.all_gather(own_rows, "dp", axis=0)
-    produced = own_schulz(whole, lax.axis_index("dp").reshape(1).astype(jnp.int32))
-    ortho = lax.all_to_all(produced, "tensor", split_axis=0, concat_axis=0, tiled=True)[:3]
     factor = 0.2 * math.sqrt(max(D, INNER))
     muon_new = jnp.stack(
         [gate_weight, inner_weight, output_weight]

time: 924 us -> 715 us (0.77)
  waiting for transfers between devices: 376 us -> 148 us
  blocking collectives: 103 us -> 129 us
    psum x1 -> x2, waiting for transfers between devices: 227 us -> 0.04 us  [the longest x1 0.02 us: local(): entry_total, readout_total = lax.psum((grad_entry, grad_readout), 'tensor')]
    unnamed x14, waiting for transfers between devices: 82.7 us -> 40.4 us
    all_gather x1, waiting for transfers between devices: 20.3 us -> 50.7 us  [local(): whole = lax.all_gather(own_rows, 'dp', axis=0)]
    psum x2, blocking collectives: 21.6 us -> 49.4 us  [the longest x1 36.9 us: local(): input_gain_sum = lax.psum(input_gain_local, ('dp', 'tensor'))]
    unnamed x335 -> x288, local copies, waits for them, and re-layouts: 42.3 us -> 51.4 us
  transfers between devices with their start and end apart: 11 -> 11, of which waited for: 6 -> 5; matrix products, arithmetic and copies ran while one was open for 19% -> 24% of each run, Pallas kernels for 16% -> 20%
where the time goes in v2:
time: 715 us; the launch traced here: 710 us
  waiting for transfers between devices  148 us (21%)
  Pallas kernels  144 us (20%)
  blocking collectives  129 us (18%)
  local copies, waits for them, and re-layouts  108 us (15%)
  matrix products  84.2 us (12%)
  other arithmetic  75.5 us (11%)
  between operations  16.1 us (2%)
    pallas_call x1, Pallas kernels, own_schulz(): pl.pallas_call(schulz_kernel, name='schulz', out_shape=jax.ShapeDtypeStru...  144 us
    unnamed x288, local copies, waits for them, and re-layouts  51.4 us
    all_gather x1, waiting for transfers between devices, local(): whole = lax.all_gather(own_rows, 'dp', axis=0)  50.7 us
    unnamed x14, waiting for transfers between devices  40.4 us
    psum x1, blocking collectives, local(): input_gain_sum = lax.psum(input_gain_local, ('dp', 'tensor'))  36.9 us
    all_to_all x1, blocking collectives, local(): lax.all_to_all(rounded_stack, 'tensor', split_axis=0, concat_axis=0, tile...  33.2 us
    all_gather x1, waiting for transfers between devices, local(): lax.all_gather(inner_weight.astype(jnp.bfloat16), 'dp', axis=0, tiled=True)  31.4 us
    psum x1, blocking collectives, local(): lax.psum((filter_local, state_filter_local, scalar_local, norm_gain_local...  25.2 us
  transfers between devices with their start and end apart: 11, of which 5 were waited for; matrix products, arithmetic and copies ran while one was open for 24% of the time, Pallas kernels for 20%

profile of v2, /device:TPU:0, one launch (start us, length us, event | category | flops | bytes accessed | tf_op | source)
XLA Modules:
  0.0 710.0 jit_solution(9317882351882460374)
XLA Ops:
  12.1 10.7 %all-gather.1 = bf16[8,192,12]{1,2,0:T(8,128)(2,1)S(1)} all-gather(bf16[1,192,12]{1,2,0:T(8,128)(2,1)S(1)} %convert_bitcast_fusion.3), channel_id=1, replica_groups=mesh['dp'=8,'tensor'=4] {'dp'}, dimensions={0}, use_global_device_ids=true | all-gather | bytes 41472 | tf_op jit(solution)/shard_map/all_gather | solution.py:386
  23.8 10.4 %all_gather.24 = bf16[1536,256]{1,0:T(8,128)(2,1)S(1)} all-gather(bf16[192,256]{1,0:T(8,128)(2,1)S(1)} %convert_element_type.126), channel_id=1, replica_groups=mesh['dp'=8,'tensor'=4] {'dp'}, dimensions={0}, use_global_device_ids=true | all-gather | bytes 884736 | tf_op jit(solution)/shard_map/all_gather | solution.py:387
  37.6 4.5 all-gather.7.cloned.1.call-done
  42.1 31.4 %all-gather.9.cloned.1.call-done = bf16[1536,768]{1,0:T(8,128)(2,1)} async-done(((bf16[192,768]{1,0:T(8,128)(2,1)}), bf16[1536,768]{1,0:T(8,128)(2,1)}) %all-gather.9.cloned.1.call-update) | async-done | bytes 2359312 | tf_op jit(solution)/shard_map/all_gather | solution.py:384
  73.5 9.8 %concatenate.37 = bf16[1536,1804]{1,0:T(8,128)(2,1)} concatenate(bf16[1536,768]{1,0:T(8,128)(2,1)} %all-gather.7.cloned.1.call-done, bf16[1536,768]{1,0:T(8,128)(2,1)} %all-gather.9.cloned.1.call-done, bf16[1536,12]{1,0:T(8,128)(2,1)} %bitcast.242, bf16[1536,256]{1,0:T(8,128)(2,1)S(1)} %all_gather.24), dimensions={1} | concatenate | bytes 11083776 | tf_op jit(solution)/shard_map/concatenate | solution.py:392
  83.3 6.1 fusion.138
  100.6 5.0 fusion.55
  116.5 11.8 %while.36 = (s32[]{:T(128)}, f32[12,64,128]{2,1,0:T(8,128)S(1)}, f32[2,12,64,128]{3,2,1,0:T(8,128)}, f32[2,12]{1,0:T(2,128)}, f32[2,12,1,1]{1,3,2,0:T(1,128)}, /...) while((s32[]{:T(128)}, f32[12,64,128]{2,1,0:T(8,128)S(1)}, ...), condition=%wide.region_5.6_spmd.clone, body=%wide.region_4.5_spmd.clone.sunk | while | flops 393243 | bytes 1968056 | solution.py:105
  131.2 7.6 %fusion.52 = f32[2,256,12,64]{1,3,2,0:T(8,128)S(1)} fusion(f32[2,12,64,256]{3,2,1,0:T(8,128)S(1)} %fusion.154, f32[2,256,256]{2,1,0:T(8,128)S(1)} %copy-done.67, f32[2,256,12]{1,2,0:T(8,128)S(1)} %copy-done.70, f32[2,256,12,64]{1,0,3,2:T(2,128)S(1)} %copy-done.4, f32[2,256,12]{1,2,0:T(8,128)S(1)} %copy-done.76, f32[2,256,12]{1,2,0:T(8,128)S(1)} %copy-done.62), kind=kOutput, calls=%fused_computation.86 | convolution fusion | flops 1213857792 | bytes 5316608 | tf_op jit(solution)/shard_map/jvp(cijh,cjhp->cihp)/dot_general | solution.py:84
  141.3 7.4 %multiply_reduce_fusion.9 = (f32[512]{0:T(512)S(1)}, f32[512]{0:T(512)S(1)}, f32[512,768]{0,1:T(8,128)}, f32[512,768]{0,1:T(8,128)}) fusion(f32[768]{0:T(1024)} %param.38, f32[512,1804]{0,1:T(8,128)} %copy-done, f32[512,768]{0,1:T(8,128)} %bitcast.231, f32[512,768]{0,1:T(8,128)} %get-tuple-element.599, f32[768]{0:T(1024)S(1)} %mul.842, ...), kind=kOutput, calls=%fused_computation.101 | convolution fusion | flops 1214249984 | bytes 11806720 | tf_op jit(solution)/shard_map/dot_general | solution.py:424
  149.3 12.6 %psum.70 = f32[2,512]{1,0:T(2,128)} all-reduce(f32[2,512]{1,0:T(2,128)} %pad_maximum_fusion.4), channel_id=1, replica_groups=mesh['dp'=8,'tensor'=4] {'tensor'}, use_global_device_ids=true, to_apply=%region_8.9 | all-reduce | flops 1024 | bytes 8192 | tf_op jit(solution)/shard_map/psum | solution.py:426
  162.6 5.8 multiply_reduce_fusion.2
  171.6 4.0 fusion.50
  175.6 10.1 %fusion.57 = (f32[2,256,12]{1,2,0:T(8,128)}, f32[2,256,12]{1,2,0:T(8,128)}, f32[2,256,256]{2,1,0:T(8,128)}) fusion(f32[2,256,12]{1,2,0:T(8,128)S(1)} %copy-done.71, f32[2,256,256]{2,1,0:T(8,128)S(1)} %copy-done.68, f32[2,256,12,64]{1,0,3,2:T(2,128)S(1)} %copy-done.4, f32[2,256,12]{1,2,0:T(8,128)S(1)} %copy-done.63, f32[2,256,12,64]{1,0,3,2:T(2,128)S(1)} %copy-done.5), kind=kOutput, calls=%fused_computation.109 | convolution fusion | flops 1228656640 | bytes 4292608 | tf_op jit(solution)/shard_map/transpose(jvp(cijh,cjhp->cihp))/dot_general | solution.py:84
  185.7 4.6 fusion.77
  194.8 13.4 %while.37 = (s32[]{:T(128)}, f32[12,64,128]{2,1,0:T(8,128)S(1)}, f32[2,12]{1,0:T(2,128)}, f32[2,12,64,128]{3,2,1,0:T(8,128)}, f32[2,12,64,128]{3,2,1,0:T(8,128)}...) while((s32[]{:T(128)}, f32[12,64,128]{2,1,0:T(8,128)S(1)}, ...), condition=%wide.region_11.12_spmd.clone, body=%wide.region_9.11_spmd.clone.sunk | while | flops 589840 | bytes 2359904 | solution.py:105
  218.7 4.4 copy.291
  223.1 6.5 bitcast_add_fusion.2
  249.9 7.4 %fusion.153 = (bf16[1536,1548]{0,1:T(8,128)(2,1)S(1)}, f32[1536,1548]{0,1:T(8,128)}) fusion(bf16[512,12]{0,1:T(8,128)(2,1)S(1)} %get-tuple-element.580, bf16[512,768]{0,1:T(8,128)(2,1)S(1)} %get-tuple-element.620, bf16[512,768]{0,1:T(8,128)(2,1)S(1)} %copy-done.34, bf16[512,1536]{1,0:T(8,128)(2,1)S(1)} %copy-done.1, f32[1536]{0:T(1024)S(1)} %copy-done.78, ...), kind=kOutput, calls=%fused_computation.276 | convolution fusion | flops 2445072384 | bytes 17432576 | tf_op jit(solution)/shard_map/td,tk->dk/dot_general | solution.py:449
  259.8 4.3 copy.289
  268.7 4.4 copy.287
  281.9 4.8 fusion.150
  286.8 36.9 %psum.77 = f32[1536]{0:T(1024)} all-reduce(f32[1536]{0:T(1024)S(1)} %get-tuple-element.611), channel_id=1, replica_groups=mesh['dp'=8,'tensor'=4] {'dp','tensor'}, use_global_device_ids=true, to_apply=%region_42.43 | all-reduce | flops 1536 | bytes 12288 | tf_op jit(solution)/shard_map/psum | solution.py:472
  323.7 25.2 %all-reduce.29 = (f32[5,768]{1,0:T(8,128)}, f32[5,256]{1,0:T(8,128)}, f32[3,12]{1,0:T(4,128)}, f32[768]{0:T(1024)}) all-reduce(f32[5,768]{1,0:T(8,128)S(1)} %pad_add_fusion.1, f32[5,256]{1,0:T(8,128)S(1)} %pad_add_fusion.2, f32[3,12]{1,0:T(4,128)S(1)} %pad_add_fusion.3, ...), channel_id=1, replica_groups=mesh['dp'=8,'tensor'=4] {'dp'}, use_global_device_ids=true, to_apply=%region_24.25 | all-reduce | flops 5924 | bytes 47392 | tf_op jit(solution)/shard_map/psum | solution.py:469
  352.3 39.7 %reduce-scatter.13.cloned.1.call-done = bf16[192,768]{1,0:T(8,128)(2,1)} async-done(((bf16[1536,768]{1,0:T(8,128)(2,1)}), bf16[192,768]{1,0:T(8,128)(2,1)}) %reduce-scatter.13.cloned.1.call-update) | async-done | bytes 294928
  399.4 33.2 %all_to_all.10 = bf16[4,192,768]{2,1,0:T(8,128)(2,1)} all-to-all(bf16[4,192,768]{2,1,0:T(8,128)(2,1)} %copy.248), channel_id=1, replica_groups=mesh['dp'=8,'tensor'=4] {'tensor'}, dimensions={0} | all-to-all | bytes 2359296 | tf_op jit(solution)/shard_map/all_to_all | solution.py:495
  433.6 4.5 convolution_convert_fusion.1
  439.0 50.7 %all-gather.13.cloned.1.call-done = bf16[32,192,768]{2,1,0:T(8,128)(2,1)} async-done(((bf16[4,192,768]{2,1,0:T(8,128)(2,1)}), bf16[32,192,768]{2,1,0:T(8,128)(2,1)}) %all-gather.13.cloned.1.call-update) | async-done | bytes 9437200 | tf_op jit(solution)/shard_map/all_gather | solution.py:496
  492.2 143.8 %schulz.1 = bf16[4,192,768]{2,1,0:T(8,128)(2,1)} custom-call(s32[1]{0:T(128)} %bitcast.60.place, bf16[8,4,192,768]{3,2,1,0:T(8,128)(2,1)} %bitcast.275), custom_call_target="tpu_custom_call" | custom-call | flops 115964116992 | bytes 18874368 | tf_op jit(solution)/shard_map/schulz/pallas_call | solution.py:324
  636.1 4.7 all-to-all-start.1
  663.4 20.7 %all-to-all-done.1 = bf16[4,192,768]{2,1,0:T(8,128)(2,1)S(1)} async-done(((bf16[4,192,768]{2,1,0:T(8,128)(2,1)}), bf16[4,192,768]{2,1,0:T(8,128)(2,1)S(1)}, u32[]{:S(2)}, u32[]{:S(2)}) %all-to-all-start.1) | async-done | bytes 1179680 | tf_op jit(solution)/shard_map/all_to_all | solution.py:507
  698.1 4.9 fusion.27
  (459 shorter events, 167.8 us)
Async XLA Ops:
  7.2 34.9 %all-gather.7.cloned.1.call-start = ((), (), s32[]{:S(2)}) async-start(), calls=%async_computation.6 | async-start | bytes 2654208 | tf_op jit(solution)/shard_map/all_gather | solution.py:383
  9.2 64.3 %all-gather.9.cloned.1.call-start = ((), (), s32[]{:S(2)}) async-start(), calls=%async_computation.7 | async-start | bytes 2654208 | tf_op jit(solution)/shard_map/all_gather | solution.py:384
  10.1 131.2 %all-gather.11.cloned.1.call-start = ((), (), s32[]{:S(2)}) async-start(), calls=%async_computation.8 | async-start | bytes 2654208 | tf_op jit(solution)/shard_map/all_gather | solution.py:385
  10.9 263.5 %all-reduce.34.cloned.1.call-start = ((), (), s32[]{:S(2)}) async-start(), calls=%async_computation.10 | async-start | bytes 1048576 | tf_op jit(solution)/shard_map/psum | solution.py:442
  12.1 99.0 %copy-start.25 = (f32[256,256]{1,0:T(8,128)}, f32[256,256]{1,0:T(8,128)S(1)}, u32[]{:S(2)}) copy-start(f32[256,256]{1,0:T(8,128)S(1)} %fusion.101) | copy-start | bytes 786436
  34.2 49.1 %copy-start.13 = (bf16[1536,256]{1,0:T(8,128)(2,1)}, bf16[1536,256]{1,0:T(8,128)(2,1)S(1)}, u32[]{:S(2)}) copy-start(bf16[1536,256]{1,0:T(8,128)(2,1)S(1)} %all_gather.24) | copy-start | bytes 2359300
  35.1 48.2 %copy-start.88 = (f32[512]{0:T(512)}, f32[512]{0:T(512)S(1)}, u32[]{:S(2)}) copy-start(f32[512]{0:T(512)S(1)} %get-tuple-element.640) | copy-start | bytes 6148
  35.1 65.4 %copy-start.82 = (f32[512]{0:T(512)}, f32[512]{0:T(512)S(1)}, u32[]{:S(2)}) copy-start(f32[512]{0:T(512)S(1)} %get-tuple-element.648) | copy-start | bytes 6148
  35.1 65.4 %copy-start.84 = (f32[512]{0:T(512)}, f32[512]{0:T(512)S(1)}, u32[]{:S(2)}) copy-start(f32[512]{0:T(512)S(1)} %get-tuple-element.646) | copy-start | bytes 6148
  35.1 65.4 %copy-start.86 = (f32[512]{0:T(512)}, f32[512]{0:T(512)S(1)}, u32[]{:S(2)}) copy-start(f32[512]{0:T(512)S(1)} %get-tuple-element.647) | copy-start | bytes 6148
  35.2 58.9 %copy-start.115 = (f32[1,256]{1,0:T(1,128)}, f32[1,256]{1,0:T(1,128)S(1)}, u32[]{:S(2)}) copy-start(f32[1,256]{1,0:T(1,128)S(1)} %get-tuple-element.635) | copy-start | bytes 3076
  35.2 58.9 %copy-start.117 = (f32[1,256]{1,0:T(1,128)}, f32[1,256]{1,0:T(1,128)S(1)}, u32[]{:S(2)}) copy-start(f32[1,256]{1,0:T(1,128)S(1)} %get-tuple-element.636) | copy-start | bytes 3076
  35.2 58.9 %copy-start.119 = (f32[1,256]{1,0:T(1,128)}, f32[1,256]{1,0:T(1,128)S(1)}, u32[]{:S(2)}) copy-start(f32[1,256]{1,0:T(1,128)S(1)} %get-tuple-element.633) | copy-start | bytes 3076
  35.2 58.9 %copy-start.121 = (f32[1,256]{1,0:T(1,128)}, f32[1,256]{1,0:T(1,128)S(1)}, u32[]{:S(2)}) copy-start(f32[1,256]{1,0:T(1,128)S(1)} %get-tuple-element.634) | copy-start | bytes 3076
  35.3 65.3 %copy-start.90 = (f32[768]{0:T(1024)}, f32[768]{0:T(1024)S(1)}, u32[]{:S(2)}) copy-start(f32[768]{0:T(1024)S(1)} %get-tuple-element.516) | copy-start | bytes 9220
  35.3 65.3 %copy-start.92 = (f32[768]{0:T(1024)}, f32[768]{0:T(1024)S(1)}, u32[]{:S(2)}) copy-start(f32[768]{0:T(1024)S(1)} %get-tuple-element.517) | copy-start | bytes 9220
  35.3 65.3 %copy-start.94 = (f32[768]{0:T(1024)}, f32[768]{0:T(1024)S(1)}, u32[]{:S(2)}) copy-start(f32[768]{0:T(1024)S(1)} %get-tuple-element.514) | copy-start | bytes 9220
  35.3 65.3 %copy-start.96 = (f32[768]{0:T(1024)}, f32[768]{0:T(1024)S(1)}, u32[]{:S(2)}) copy-start(f32[768]{0:T(1024)S(1)} %get-tuple-element.515) | copy-start | bytes 9220
  37.4 60.2 %copy-start.125 = (f32[12]{0:T(128)}, f32[12]{0:T(128)S(1)}, u32[]{:S(2)}) copy-start(f32[12]{0:T(128)S(1)} %get-tuple-element.642) | copy-start | bytes 148
  37.4 60.2 %copy-start.127 = (f32[12]{0:T(128)}, f32[12]{0:T(128)S(1)}, u32[]{:S(2)}) copy-start(f32[12]{0:T(128)S(1)} %get-tuple-element.643) | copy-start | bytes 148
  37.5 72.3 %copy-start.100 = (f32[2,256]{1,0:T(2,128)}, f32[2,256]{1,0:T(2,128)S(1)}, u32[]{:S(2)}) copy-start(f32[2,256]{1,0:T(2,128)S(1)} %get-tuple-element.645) | copy-start | bytes 6148
  37.5 72.3 %copy-start.105 = (f32[2,256]{1,0:T(2,128)}, f32[2,256]{1,0:T(2,128)S(1)}, u32[]{:S(2)}) copy-start(f32[2,256]{1,0:T(2,128)S(1)} %get-tuple-element.644) | copy-start | bytes 6148
  37.6 125.0 %copy-start.98 = (f32[768]{0:T(1024)}, f32[768]{0:T(1024)S(1)}, u32[]{:S(2)}) copy-start(f32[768]{0:T(1024)S(1)} %mul.842) | copy-start | bytes 9220
  218.6 130.2 %reduce-scatter.17.cloned.1.call-start = ((), (), s32[]{:S(2)}) async-start(), calls=%async_computation.13 | async-start | bytes 2654208
  236.2 113.8 %reduce-scatter.15.cloned.1.call-start = ((), (), s32[]{:S(2)}) async-start(), calls=%async_computation.12 | async-start | bytes 2654208
  264.1 127.8 %reduce-scatter.13.cloned.1.call-start = ((), (), s32[]{:S(2)}) async-start(), calls=%async_computation.11 | async-start | bytes 2654208
  274.0 215.6 %all-gather.13.cloned.1.call-start = ((), (), s32[]{:S(2)}) async-start(), calls=%async_computation.9 | async-start | bytes 10616832 | tf_op jit(solution)/shard_map/all_gather | solution.py:496
  349.9 43.1 %copy-start.27 = (bf16[192,768]{0,1:T(8,128)(2,1)}, bf16[192,768]{0,1:T(8,128)(2,1)S(1)}, u32[]{:S(2)}) copy-start(bf16[192,768]{0,1:T(8,128)(2,1)S(1)} %copy.292) | copy-start | bytes 884740
  351.2 41.9 %copy-start.29 = (bf16[192,768]{0,1:T(8,128)(2,1)}, bf16[192,768]{0,1:T(8,128)(2,1)S(1)}, u32[]{:S(2)}) copy-start(bf16[192,768]{0,1:T(8,128)(2,1)S(1)} %copy.290) | copy-start | bytes 884740
  432.6 254.3 %reduce-scatter.19.cloned.1.call-start = ((), (), s32[]{:S(2)}) async-start(), calls=%async_computation.14 | async-start | bytes 2654208
  491.6 196.5 %all-reduce.36.cloned.1.call-start = ((), (), s32[]{:S(2)}) async-start(), calls=%async_computation.15 | async-start | bytes 6291456 | tf_op jit(solution)/shard_map/psum | solution.py:501
  636.1 48.0 %all-to-all-start.1 = ((bf16[4,192,768]{2,1,0:T(8,128)(2,1)}), bf16[4,192,768]{2,1,0:T(8,128)(2,1)S(1)}, u32[]{:S(2)}, u32[]{:S(2)}) async-start(bf16[4,192,768]{2,1,0:T(8,128)(2,1)} %schulz.1), calls=%async_computation.1 | async-start | bytes 2359296 | tf_op jit(solution)/shard_map/all_to_all | solution.py:507
  (110 other events, 583.7 us)
Sparse Core Ops, SparseCore 0:
  10.5 31.5 all-gather.6
  44.6 28.8 all-gather.8
  76.0 28.8 all-gather.10
  218.7 35.8 all-reduce.33
  257.8 42.2 reduce-scatter.16
  303.3 42.9 reduce-scatter.14
  349.6 42.2 reduce-scatter.12
  432.8 56.8 all-gather.12
  493.0 42.3 reduce-scatter.18
  538.2 141.1 all-reduce.35

commit v3 on v2

--- a/solution.py
+++ b/solution.py
@@ -49,7 +49,6 @@
 
 
 def state_mixer(
-    gate_part,
     inner_part,
     delta_raw,
     entry_rows,
@@ -112,7 +111,7 @@
     outputs = (within + carried).reshape(row_count, head_count, head_width) + head_scalars[2][
         None, :, None
     ] * heads_in
-    return outputs.reshape(row_count, head_count * head_width) * jax.nn.silu(gate_part)
+    return outputs.reshape(row_count, head_count * head_width)
 
 
 def schulz_kernel(
@@ -379,17 +378,13 @@
 ):
     row_count = tokens.shape[0]
     segment, position = packing_layout(lengths[0], row_count)
-    full_gate, full_inner, full_output, full_delta, full_state = (
-        lax.all_gather(gate_weight.astype(jnp.bfloat16), "dp", axis=0, tiled=True),
-        lax.all_gather(inner_weight.astype(jnp.bfloat16), "dp", axis=0, tiled=True),
-        lax.all_gather(output_weight.astype(jnp.bfloat16), "dp", axis=0, tiled=True),
-        lax.all_gather(delta_weight.astype(jnp.bfloat16), "dp", axis=0, tiled=True),
-        lax.all_gather(state_weight.astype(jnp.bfloat16), "dp", axis=0, tiled=True),
-    )
-    columns = full_gate.shape[1]
-    head_count = full_delta.shape[1]
+    columns = gate_weight.shape[1]
+    head_count = delta_weight.shape[1]
     mixing_cols = 2 * columns + head_count
-    in_matrix = jnp.concatenate([full_gate, full_inner, full_delta, full_state], axis=1)
+    in_rows = jnp.concatenate([gate_weight, inner_weight, delta_weight, state_weight], axis=1)
+    in_matrix = lax.all_gather(in_rows.astype(jnp.bfloat16), "dp", axis=0, tiled=True)
+    full_output = lax.all_gather(output_weight.astype(jnp.bfloat16), "dp", axis=0, tiled=True)
+    full_state = in_matrix[:, mixing_cols:]
     tokens_wide = tokens.astype(jnp.float32)
     root_scale = lax.rsqrt(
         jnp.mean(tokens_wide * tokens_wide, axis=1, keepdims=True) + norm_epsilon
@@ -405,15 +400,14 @@
         filtered = causal_filter(raw_values, taps, position)
         return (filtered[:, :NSTATE], filtered[:, NSTATE:])
 
-    def mixer(gate_in, inner_in, delta_in, entry_in, readout_in, taps, scalars):
+    def mixer(inner_in, delta_in, entry_in, readout_in, taps, scalars):
         return state_mixer(
-            gate_in, inner_in, delta_in, entry_in, readout_in, taps, scalars, segment, position
+            inner_in, delta_in, entry_in, readout_in, taps, scalars, segment, position
         )
 
     (entry_rows, readout_rows), state_back = jax.vjp(state_rows, state_raw, state_filter)
-    gated, mixer_back = jax.vjp(
+    mixed_rows, mixer_back = jax.vjp(
         mixer,
-        gate_part,
         inner_part,
         delta_raw,
         entry_rows,
@@ -421,6 +415,9 @@
         inner_filter,
         head_scalars,
     )
+    gate_sigmoid = jax.nn.sigmoid(gate_part)
+    gate_silu = gate_part * gate_sigmoid
+    gated = mixed_rows * gate_silu
     grad_normalized = jnp.dot(cotangent, full_output, preferred_element_type=jnp.float32)
     weighted = grad_normalized * norm_gain
     squares, inner_dot = lax.psum(
@@ -436,19 +433,42 @@
     )
     norm_gain_local = jnp.sum(grad_normalized * gated * norm_scale, axis=0)
     grad_gated = norm_scale * weighted - gated * norm_scale**3 * (inner_dot / INNER)[:, None]
-    grad_gate, grad_inner, grad_delta, grad_entry, grad_readout, filter_local, scalar_local = (
-        mixer_back(grad_gated)
-    )
+    grad_gate = (
+        grad_gated * mixed_rows * (gate_sigmoid + gate_silu * (1.0 - gate_sigmoid))
+    ).astype(jnp.bfloat16)
+
+    def weight_gradient(columns_grad):
+        return jnp.einsum("td,tk->dk", normed, columns_grad, preferred_element_type=jnp.float32)
+
+    def scattered(partial):
+        low = partial.astype(jnp.bfloat16)
+        return lax.psum_scatter(low, "dp", scatter_dimension=0, tiled=True)
+
+    output_low, gate_low, grad_mixed = lax.optimization_barrier(
+        (
+            output_local.astype(jnp.bfloat16),
+            weight_gradient(grad_gate).astype(jnp.bfloat16),
+            grad_gated * gate_silu,
+        )
+    )
+    output_sum = scattered(output_low)
+    gate_sum = scattered(gate_low)
+    grad_inner, grad_delta, grad_entry, grad_readout, filter_local, scalar_local = mixer_back(
+        grad_mixed
+    )
+    grad_inner = grad_inner.astype(jnp.bfloat16)
+    inner_sum = scattered(weight_gradient(grad_inner))
     entry_total, readout_total = lax.psum((grad_entry, grad_readout), "tensor")
+    entry_total, readout_total, _, _, _ = lax.optimization_barrier(
+        (entry_total, readout_total, output_sum, gate_sum, inner_sum)
+    )
     grad_state, state_filter_local = state_back((entry_total, readout_total))
-    grad_mixing = jnp.concatenate([grad_gate, grad_inner, grad_delta], axis=1).astype(jnp.bfloat16)
+    grad_delta = grad_delta.astype(jnp.bfloat16)
+    grad_mixing = jnp.concatenate([grad_gate, grad_inner, grad_delta], axis=1)
     grad_state_low = grad_state.astype(jnp.bfloat16)
     input_partial = jnp.einsum(
         "tk,dk->td", grad_mixing, in_matrix[:, :mixing_cols], preferred_element_type=jnp.float32
     )
-    mixing_weight_grad = jnp.einsum(
-        "td,tk->dk", normed, grad_mixing, preferred_element_type=jnp.float32
-    )
     state_local = jnp.einsum(
         "td,tk->dk", normed, grad_state_low, preferred_element_type=jnp.float32
     )
@@ -459,52 +479,59 @@
         (input_partial + state_input / lax.axis_size("tensor")) * tokens_wide * root_scale, axis=0
     )
 
-    def scattered(partial):
-        low = partial.astype(jnp.bfloat16)
-        return lax.psum_scatter(low, "dp", scatter_dimension=0, tiled=True).astype(jnp.float32)
-
-    output_sum = scattered(output_local)
-    gate_sum = scattered(mixing_weight_grad[:, :columns])
-    inner_sum = scattered(mixing_weight_grad[:, columns : 2 * columns])
-    filter_sum, state_filter_sum, scalar_sum, norm_gain_sum = lax.psum(
-        (filter_local, state_filter_local, scalar_local, norm_gain_local), "dp"
-    )
-    input_gain_sum = lax.psum(input_gain_local, ("dp", "tensor"))
+    output_sum, gate_sum, inner_sum = (
+        total.astype(jnp.float32) for total in (output_sum, gate_sum, inner_sum)
+    )
     fresh_stack = moment_decay * jnp.stack([gate_moment, inner_moment, output_moment]) + jnp.stack(
         [gate_sum, inner_sum, output_sum]
     )
     spare = jnp.zeros((lax.axis_size("tensor") - 3,) + fresh_stack.shape[1:], jnp.bfloat16)
     rounded_stack = jnp.concatenate([fresh_stack.astype(jnp.bfloat16), spare], axis=0)
-    (
-        rounded_stack,
-        filter_sum,
-        state_filter_sum,
-        scalar_sum,
-        norm_gain_sum,
-        input_gain_sum,
-    ) = lax.optimization_barrier(
-        (
-            rounded_stack,
-            filter_sum,
-            state_filter_sum,
-            scalar_sum,
-            norm_gain_sum,
-            input_gain_sum,
-        )
-    )
+    filter_sum, scalar_sum, norm_gain_sum = lax.psum(
+        (filter_local, scalar_local, norm_gain_local), "dp"
+    )
+    rounded_stack, filter_sum, scalar_sum, norm_gain_sum = lax.optimization_barrier(
+        (rounded_stack, filter_sum, scalar_sum, norm_gain_sum)
+    )
+    input_gain_local = lax.psum(input_gain_local, "tensor")
     own_rows = lax.all_to_all(rounded_stack, "tensor", split_axis=0, concat_axis=0, tiled=True)
     whole = lax.all_gather(own_rows, "dp", axis=0)
-    side = jnp.concatenate([state_local, mixing_weight_grad[:, 2 * columns :]], axis=1)
-    whole, out_low, input_low, side = lax.optimization_barrier(
-        (whole, partial_out.astype(jnp.bfloat16), input_partial.astype(jnp.bfloat16), side)
+    side = jnp.concatenate([state_local, weight_gradient(grad_delta)], axis=1)
+    whole, out_low, input_low, side, input_gain_local = lax.optimization_barrier(
+        (
+            whole,
+            partial_out.astype(jnp.bfloat16),
+            input_partial.astype(jnp.bfloat16),
+            side.astype(jnp.bfloat16),
+            input_gain_local,
+        )
     )
     out_total, input_total = lax.psum((out_low, input_low), "tensor")
     side_sum = lax.psum_scatter(side, "dp", scatter_dimension=0, tiled=True)
     produced = own_schulz(whole, lax.axis_index("dp").reshape(1).astype(jnp.int32))
-    out_total, input_total, side_sum, _ = lax.optimization_barrier(
-        (out_total, input_total, side_sum, produced[0, :16, :128])
+    (
+        out_total,
+        input_total,
+        side_sum,
+        state_filter_local,
+        input_gain_local,
+        _,
+    ) = lax.optimization_barrier(
+        (
+            out_total,
+            input_total,
+            side_sum,
+            state_filter_local,
+            input_gain_local,
+            produced[0, :16, :128],
+        )
     )
     ortho = lax.all_to_all(produced, "tensor", split_axis=0, concat_axis=0, tiled=True)[:3]
+    state_filter_sum, input_gain_sum = lax.psum((state_filter_local, input_gain_local), "dp")
+    ortho, state_filter_sum, input_gain_sum = lax.optimization_barrier(
+        (ortho, state_filter_sum, input_gain_sum)
+    )
+    side_sum = side_sum.astype(jnp.float32)
     state_sum = side_sum[:, : 2 * NSTATE]
     delta_sum = side_sum[:, 2 * NSTATE :]
     block_output = (tokens_wide + out_total.astype(jnp.float32)).astype(jnp.bfloat16)

time: 715 us -> 654 us (0.915)
  blocking collectives: 129 us -> 71.5 us
  local copies, waits for them, and re-layouts: 108 us -> 82.1 us
  waiting for transfers between devices: 148 us -> 161 us
    all_to_all x1 -> x0, blocking collectives: 33.2 us -> none  [local(): lax.all_to_all(rounded_stack, 'tensor', split_axis=0, concat_axis=0, tile...]
    all_to_all x0 -> x1, waiting for transfers between devices: none -> 26.1 us  [local(): lax.all_to_all(rounded_stack, 'tensor', split_axis=0, concat_axis=0, tile...]
    all_gather x2 -> x0, blocking collectives: 21.1 us -> none  [the longest x1 10.7 us: local(): lax.all_gather(delta_weight.astype(jnp.bfloat16), 'dp', axis=0, tiled=True)]
    all_gather x1, waiting for transfers between devices: 50.7 us -> 31.4 us  [local(): whole = lax.all_gather(own_rows, 'dp', axis=0)]
    psum x1, waiting for transfers between devices: 0.02 us -> 12.2 us  [local(): entry_total, readout_total = lax.psum((grad_entry, grad_readout), 'tensor')]
    unnamed x14 -> x13, waiting for transfers between devices: 40.4 us -> 28.4 us
    unnamed x288 -> x315, local copies, waits for them, and re-layouts: 51.4 us -> 41.1 us
    concatenate x1, local copies, waits for them, and re-layouts: 9.77 us -> 1.04 us  [local(): jnp.concatenate([gate_weight, inner_weight, delta_weight, state_weight],...]
  transfers between devices with their start and end apart: 11 -> 11, of which waited for: 5 -> 6; matrix products, arithmetic and copies ran while one was open for 24% -> 28% of each run, Pallas kernels for 20% -> 22%
where the time goes in v3:
time: 654 us; the launch traced here: 647 us
  waiting for transfers between devices  161 us (25%)
  Pallas kernels  144 us (22%)
  matrix products  84.3 us (13%)
  local copies, waits for them, and re-layouts  82.1 us (13%)
  other arithmetic  77.5 us (12%)
  blocking collectives  71.5 us (11%)
  between operations  15.9 us (2%)
  starting transfers between devices  10.5 us (2%)
    pallas_call x1, Pallas kernels, own_schulz(): pl.pallas_call(schulz_kernel, name='schulz', out_shape=jax.ShapeDtypeStru...  144 us
    unnamed x315, local copies, waits for them, and re-layouts  41.1 us
    all_gather x1, waiting for transfers between devices, local(): lax.all_gather(in_rows.astype(jnp.bfloat16), 'dp', axis=0, tiled=True)  38.8 us
    all_gather x1, waiting for transfers between devices, local(): whole = lax.all_gather(own_rows, 'dp', axis=0)  31.4 us
    unnamed x13, waiting for transfers between devices  28.4 us
    all_to_all x1, waiting for transfers between devices, local(): lax.all_to_all(rounded_stack, 'tensor', split_axis=0, concat_axis=0, tile...  26.1 us
    psum x1, blocking collectives, local(): lax.psum((state_filter_local, input_gain_local), 'dp')  24.6 us
    all_to_all x1, waiting for transfers between devices, local(): lax.all_to_all(produced, 'tensor', split_axis=0, concat_axis=0, tiled=True)  23.7 us
  transfers between devices with their start and end apart: 11, of which 6 were waited for; matrix products, arithmetic and copies ran while one was open for 28% of the time, Pallas kernels for 22%

profile of v3, /device:TPU:0, one launch (start us, length us, event | category | flops | bytes accessed | tf_op | source)
XLA Modules:
  0.0 646.7 jit_solution(8347721677594392626)
XLA Ops:
  19.2 38.8 %all-gather.5.cloned.1.call-done = bf16[1536,1804]{1,0:T(8,128)(2,1)} async-done(((bf16[192,1804]{1,0:T(8,128)(2,1)}), bf16[1536,1804]{1,0:T(8,128)(2,1)}) %all-gather.5.cloned.1.call-update) | async-done | bytes 5541904 | tf_op jit(solution)/shard_map/all_gather | solution.py:385
  58.0 6.0 fusion.136
  73.6 5.2 fusion.52
  85.8 8.6 %while.36 = (s32[]{:T(128)}, f32[12,64,128]{2,1,0:T(8,128)S(1)}, f32[2,12,64,128]{3,2,1,0:T(8,128)S(1)}, f32[2,12]{1,0:T(2,128)S(1)}, f32[2,12,1,1]{1,3,2,0:T(1,...) while((s32[]{:T(128)}, f32[12,64,128]{2,1,0:T(8,128)S(1)}, ...), condition=%wide.region_5.6_spmd.clone, body=%wide.region_4.5_spmd.clone.sunk | while | flops 393243 | bytes 1967592 | solution.py:104
  95.9 7.6 %fusion.50 = f32[2,256,12,64]{1,3,2,0:T(8,128)S(1)} fusion(f32[2,12,64,256]{3,2,1,0:T(8,128)S(1)} %fusion.148, f32[2,256,256]{2,1,0:T(8,128)S(1)} %copy-done.63, f32[2,256,12]{1,2,0:T(8,128)S(1)} %convolution_bitcast_fusion.1, f32[2,256,12,64]{1,0,3,2:T(2,128)S(1)} %reshape.402, f32[2,256,12]{1,2,0:T(8,128)S(1)} %get-tuple-element.648, ...), kind=kOutput, calls=%fused_computation.85 | convolution fusion | flops 1213857792 | bytes 5316608 | tf_op jit(solution)/shard_map/jvp(cijh,cjhp->cihp)/dot_general | solution.py:83
  106.8 7.0 %multiply_reduce_fusion.9 = (f32[512]{0:T(512)S(1)}, f32[512]{0:T(512)S(1)}, f32[512,768]{0,1:T(8,128)}, f32[512,768]{0,1:T(8,128)}) fusion(f32[768]{0:T(1024)} %param.38, f32[512,1804]{0,1:T(8,128)} %copy-done, f32[512,768]{0,1:T(8,128)} %bitcast.230, f32[512,768]{0,1:T(8,128)S(1)} %copy-done.15, f32[768]{0:T(1024)S(1)} %copy-done.95, ...), kind=kOutput, calls=%fused_computation.101 | convolution fusion | flops 1214249984 | bytes 11806720 | tf_op jit(solution)/shard_map/dot_general | solution.py:421
  114.4 12.4 %psum.77 = f32[2,512]{1,0:T(2,128)} all-reduce(f32[2,512]{1,0:T(2,128)} %pad_maximum_fusion.1), channel_id=1, replica_groups=mesh['dp'=8,'tensor'=4] {'tensor'}, use_global_device_ids=true, to_apply=%region_8.9 | all-reduce | flops 1024 | bytes 8192 | tf_op jit(solution)/shard_map/psum | solution.py:423
  127.6 4.9 fusion.33
  132.5 4.5 fusion.79
  138.0 3.1 convolution_convert_fusion.1
  143.6 3.4 fusion.48
  148.5 12.9 %while.37 = (s32[]{:T(128)}, f32[12,64,128]{2,1,0:T(8,128)S(1)}, f32[2,12]{1,0:T(2,128)}, f32[2,12,64,128]{3,2,1,0:T(8,128)}, f32[2,12,64,128]{3,2,1,0:T(8,128)}...) while((s32[]{:T(128)}, f32[12,64,128]{2,1,0:T(8,128)S(1)}, ...), condition=%wide.region_12.13_spmd.clone, body=%wide.region_10.12_spmd.clone.sunk | while | flops 589840 | bytes 2360316 | solution.py:104
  164.2 5.5 bitcast_add_fusion.2
  181.8 3.1 convolution_convert_fusion
  185.0 4.5 copy.294
  198.5 10.1 %fusion.54 = (f32[2,256,12]{1,2,0:T(8,128)S(1)}, f32[2,256,12]{1,2,0:T(8,128)S(1)}, f32[2,256,256]{2,1,0:T(8,128)}) fusion(f32[2,256,12]{1,2,0:T(8,128)S(1)} %copy-done.67, f32[2,256,256]{2,1,0:T(8,128)S(1)} %copy-done.65, f32[2,256,12,64]{1,0,3,2:T(2,128)S(1)} %reshape.402, f32[2,256,12]{1,2,0:T(8,128)S(1)} %copy-done.59, f32[2,256,12,64]{1,0,3,2:T(2,128)S(1)} %reshape.407), kind=kOutput, calls=%fused_computation.108 | convolution fusion | flops 1228656640 | bytes 4292608 | tf_op jit(solution)/shard_map/transpose(jvp(cijh,cjhp->cihp))/dot_general | solution.py:83
  215.3 23.2 %all-reduce.30 = (f32[5,768]{1,0:T(8,128)}, f32[3,12]{1,0:T(4,128)}, f32[768]{0:T(1024)}) all-reduce(f32[5,768]{1,0:T(8,128)S(1)} %pad_add_fusion, f32[3,12]{1,0:T(4,128)S(1)} %pad_add_fusion.2, f32[768]{0:T(1024)S(1)} %copy-done.109), channel_id=1, replica_groups=mesh['dp'=8,'tensor'=4] {'dp'}, use_global_device_ids=true, to_apply=%region_20.21 | all-reduce | flops 4644 | bytes 37152 | tf_op jit(solution)/shard_map/psum | solution.py:490
  244.5 27.6 %reduce-scatter.17.cloned.1.call-done = bf16[192,768]{1,0:T(8,128)(2,1)} async-done(((bf16[1536,768]{1,0:T(8,128)(2,1)}), bf16[192,768]{1,0:T(8,128)(2,1)}) %reduce-scatter.17.cloned.1.call-update) | async-done | bytes 294928
  275.3 3.6 fusion.143
  282.7 4.7 all-to-all-start
  288.0 3.9 fusion.71
  298.3 26.1 %all-to-all-done = bf16[4,192,768]{2,1,0:T(8,128)(2,1)} async-done(((bf16[4,192,768]{2,1,0:T(8,128)(2,1)}), bf16[4,192,768]{2,1,0:T(8,128)(2,1)}, u32[]{:S(2)}, u32[]{:S(2)}) %all-to-all-start) | async-done | bytes 1179680 | tf_op jit(solution)/shard_map/all_to_all | solution.py:497
  326.1 4.5 convolution_convert_fusion.3
  330.6 12.2 %all-reduce.36.cloned.1.call-done = (f32[512,128]{0,1:T(8,128)}, f32[512,128]{0,1:T(8,128)}) async-done(((f32[512,128]{0,1:T(8,128)}, f32[512,128]{0,1:T(8,128)}), (f32[512,128]{0,1:T(8,128)}, f32[512,128]{0,1:T(8,128)})) %all-reduce.36.cloned.1.call-update) | async-done | bytes 524304 | tf_op jit(solution)/shard_map/psum | solution.py:461
  351.2 8.7 %fusion.20 = (f32[1536]{0:T(1024)S(1)}, bf16[512,1536]{1,0:T(8,128)(2,1)}) fusion(bf16[512,1536]{1,0:T(8,128)(2,1)S(1)} %copy-done.8, f32[512,1536]{1,0:T(8,128)S(1)} %fusion.77, f32[512]{0:T(512)S(1)} %copy-done.125, bf16[1536,1804]{1,0:T(8,128)(2,1)} %all-gather.5.cloned.1.call-done, bf16[512,12]{0,1:T(8,128)(2,1)S(1)} %copy-done.110, ...), kind=kOutput, calls=%fused_computation.41 | convolution fusion | flops 2445052416 | bytes 12996608 | tf_op jit(solution)/shard_map/tk,dk->td/dot_general | solution.py:469
  359.8 11.3 %psum.83 = f32[1536]{0:T(1024)} all-reduce(f32[1536]{0:T(1024)S(1)} %get-tuple-element.628), channel_id=1, replica_groups=mesh['dp'=8,'tensor'=4] {'tensor'}, use_global_device_ids=true, to_apply=%region_36.37 | all-reduce | flops 1536 | bytes 12288 | tf_op jit(solution)/shard_map/psum | solution.py:496
  371.9 31.4 %all-gather.9.cloned.1.call-done = bf16[32,192,768]{2,1,0:T(8,128)(2,1)} async-done(((bf16[4,192,768]{2,1,0:T(8,128)(2,1)}), bf16[32,192,768]{2,1,0:T(8,128)(2,1)}) %all-gather.9.cloned.1.call-update) | async-done | bytes 9437200 | tf_op jit(solution)/shard_map/all_gather | solution.py:498
  405.5 144.2 %schulz.1 = bf16[4,192,768]{2,1,0:T(8,128)(2,1)} custom-call(s32[1]{0:T(128)} %bitcast.56.place, bf16[8,4,192,768]{3,2,1,0:T(8,128)(2,1)} %bitcast.272), custom_call_target="tpu_custom_call" | custom-call | flops 115964116992 | bytes 18874368 | tf_op jit(solution)/shard_map/schulz/pallas_call | solution.py:323
  549.7 4.8 all-to-all-start.1
  568.6 23.7 %all-to-all-done.1 = bf16[4,192,768]{2,1,0:T(8,128)(2,1)} async-done(((bf16[4,192,768]{2,1,0:T(8,128)(2,1)}), bf16[4,192,768]{2,1,0:T(8,128)(2,1)}, u32[]{:S(2)}, u32[]{:S(2)}) %all-to-all-start.1) | async-done | bytes 1179680 | tf_op jit(solution)/shard_map/all_to_all | solution.py:529
  599.1 24.6 %all-reduce.29 = (f32[5,256]{1,0:T(8,128)}, f32[1536]{0:T(1024)}) all-reduce(f32[5,256]{1,0:T(8,128)} %pad_add_fusion.1, f32[1536]{0:T(1024)} %psum.83), channel_id=1, replica_groups=mesh['dp'=8,'tensor'=4] {'dp'}, use_global_device_ids=true, to_apply=%region_46.47 | all-reduce | flops 2816 | bytes 22528 | tf_op jit(solution)/shard_map/psum | solution.py:530
  637.0 3.0 fusion.23
  (491 shorter events, 157.1 us)
Async XLA Ops:
  7.2 50.8 %all-gather.5.cloned.1.call-start = ((), (), s32[]{:S(2)}) async-start(), calls=%async_computation.6 | async-start | bytes 6635520 | tf_op jit(solution)/shard_map/all_gather | solution.py:385
  11.4 46.6 %copy-start.74 = (f32[1536]{0:T(1024)S(1)}, f32[1536]{0:T(1024)}, u32[]{:S(2)}) copy-start(f32[1536]{0:T(1024)} %param.39) | copy-start | bytes 18436
  11.4 94.7 %all-gather.7.cloned.1.call-start = ((), (), s32[]{:S(2)}) async-start(), calls=%async_computation.7 | async-start | bytes 2654208 | tf_op jit(solution)/shard_map/all_gather | solution.py:386
  12.2 226.2 %reduce-scatter.13.cloned.1.call-start = ((), (), s32[]{:S(2)}) async-start(), calls=%async_computation.9 | async-start | bytes 2654208
  14.1 54.3 %copy-start.132 = (f32[12]{0:T(128)}, f32[12]{0:T(128)S(1)}, u32[]{:S(2)}) copy-start(f32[12]{0:T(128)S(1)} %get-tuple-element.660) | copy-start | bytes 148
  14.1 54.3 %copy-start.134 = (f32[12]{0:T(128)}, f32[12]{0:T(128)S(1)}, u32[]{:S(2)}) copy-start(f32[12]{0:T(128)S(1)} %get-tuple-element.661) | copy-start | bytes 148
  15.1 48.9 %copy-start.122 = (f32[512]{0:T(512)}, f32[512]{0:T(512)S(1)}, u32[]{:S(2)}) copy-start(f32[512]{0:T(512)S(1)} %get-tuple-element.658) | copy-start | bytes 6148
  17.8 64.0 %copy-start.97 = (f32[2,256]{1,0:T(2,128)}, f32[2,256]{1,0:T(2,128)S(1)}, u32[]{:S(2)}) copy-start(f32[2,256]{1,0:T(2,128)S(1)} %get-tuple-element.663) | copy-start | bytes 6148
  17.8 55.8 %copy-start.77 = (f32[512]{0:T(512)}, f32[512]{0:T(512)S(1)}, u32[]{:S(2)}) copy-start(f32[512]{0:T(512)S(1)} %get-tuple-element.664) | copy-start | bytes 6148
  17.8 55.8 %copy-start.79 = (f32[512]{0:T(512)}, f32[512]{0:T(512)S(1)}, u32[]{:S(2)}) copy-start(f32[512]{0:T(512)S(1)} %get-tuple-element.665) | copy-start | bytes 6148
  17.8 55.8 %copy-start.82 = (f32[512]{0:T(512)}, f32[512]{0:T(512)S(1)}, u32[]{:S(2)}) copy-start(f32[512]{0:T(512)S(1)} %get-tuple-element.666) | copy-start | bytes 6148
  18.4 50.8 %copy-start.111 = (f32[1,256]{1,0:T(1,128)}, f32[1,256]{1,0:T(1,128)S(1)}, u32[]{:S(2)}) copy-start(f32[1,256]{1,0:T(1,128)S(1)} %get-tuple-element.653) | copy-start | bytes 3076
  18.4 50.8 %copy-start.113 = (f32[1,256]{1,0:T(1,128)}, f32[1,256]{1,0:T(1,128)S(1)}, u32[]{:S(2)}) copy-start(f32[1,256]{1,0:T(1,128)S(1)} %get-tuple-element.652) | copy-start | bytes 3076
  19.2 54.4 %copy-start.87 = (f32[768]{0:T(1024)}, f32[768]{0:T(1024)S(1)}, u32[]{:S(2)}) copy-start(f32[768]{0:T(1024)S(1)} %get-tuple-element.534) | copy-start | bytes 9220
  19.2 54.4 %copy-start.89 = (f32[768]{0:T(1024)}, f32[768]{0:T(1024)S(1)}, u32[]{:S(2)}) copy-start(f32[768]{0:T(1024)S(1)} %get-tuple-element.535) | copy-start | bytes 9220
  19.2 54.4 %copy-start.91 = (f32[768]{0:T(1024)}, f32[768]{0:T(1024)S(1)}, u32[]{:S(2)}) copy-start(f32[768]{0:T(1024)S(1)} %get-tuple-element.533) | copy-start | bytes 9220
  19.2 54.4 %copy-start.93 = (f32[768]{0:T(1024)}, f32[768]{0:T(1024)S(1)}, u32[]{:S(2)}) copy-start(f32[768]{0:T(1024)S(1)} %get-tuple-element.532) | copy-start | bytes 9220
  69.1 26.8 %copy-start.58 = (f32[2,256,12]{1,2,0:T(8,128)}, f32[2,256,12]{1,2,0:T(8,128)S(1)}, u32[]{:S(2)}) copy-start(f32[2,256,12]{1,2,0:T(8,128)S(1)} %copy.226) | copy-start | bytes 73732
  141.1 98.5 %reduce-scatter.15.cloned.1.call-start = ((), (), s32[]{:S(2)}) async-start(), calls=%async_computation.10 | async-start | bytes 2654208
  184.9 87.2 %reduce-scatter.17.cloned.1.call-start = ((), (), s32[]{:S(2)}) async-start(), calls=%async_computation.11 | async-start | bytes 2654208
  239.6 34.4 %copy-start.30 = (bf16[192,768]{0,1:T(8,128)(2,1)}, bf16[192,768]{0,1:T(8,128)(2,1)S(1)}, u32[]{:S(2)}) copy-start(bf16[192,768]{0,1:T(8,128)(2,1)S(1)} %copy.291) | copy-start | bytes 884740
  282.7 41.6 %all-to-all-start = ((bf16[4,192,768]{2,1,0:T(8,128)(2,1)}), bf16[4,192,768]{2,1,0:T(8,128)(2,1)}, u32[]{:S(2)}, u32[]{:S(2)}) async-start(bf16[4,192,768]{2,1,0:T(8,128)(2,1)} %copy.246), calls=%async_computation | async-start | bytes 2359296 | tf_op jit(solution)/shard_map/all_to_all | solution.py:497
  287.5 55.4 %all-reduce.36.cloned.1.call-start = ((), (), s32[]{:S(2)}) async-start(), calls=%async_computation.13 | async-start | bytes 1048576 | tf_op jit(solution)/shard_map/psum | solution.py:461
  296.6 28.0 %copy-start.8 = (bf16[512,1536]{1,0:T(8,128)(2,1)S(1)}, bf16[512,1536]{1,0:T(8,128)(2,1)}, u32[]{:S(2)}) copy-start(bf16[512,1536]{1,0:T(8,128)(2,1)} %param.27) | copy-start | bytes 4718596
  296.6 28.0 %copy-start.110 = (bf16[512,12]{0,1:T(8,128)(2,1)S(1)}, bf16[512,12]{0,1:T(8,128)(2,1)}, u32[]{:S(2)}) copy-start(bf16[512,12]{0,1:T(8,128)(2,1)} %get-tuple-element.605) | copy-start | bytes 36868
  296.6 28.0 %copy-start.125 = (f32[512]{0:T(512)S(1)}, f32[512]{0:T(512)}, u32[]{:S(2)}) copy-start(f32[512]{0:T(512)} %copy-done.122) | copy-start | bytes 6148
  298.2 105.1 %all-gather.9.cloned.1.call-start = ((), (), s32[]{:S(2)}) async-start(), calls=%async_computation.8 | async-start | bytes 10616832 | tf_op jit(solution)/shard_map/all_gather | solution.py:498
  324.4 243.2 %reduce-scatter.19.cloned.1.call-start = ((), (), s32[]{:S(2)}) async-start(), calls=%async_computation.12 | async-start | bytes 1327104
  404.7 189.7 %all-reduce.38.cloned.1.call-start = ((), (), s32[]{:S(2)}) async-start(), calls=%async_computation.14 | async-start | bytes 6291456 | tf_op jit(solution)/shard_map/psum | solution.py:509
  549.7 42.6 %all-to-all-start.1 = ((bf16[4,192,768]{2,1,0:T(8,128)(2,1)}), bf16[4,192,768]{2,1,0:T(8,128)(2,1)}, u32[]{:S(2)}, u32[]{:S(2)}) async-start(bf16[4,192,768]{2,1,0:T(8,128)(2,1)} %schulz.1), calls=%async_computation.1 | async-start | bytes 2359296 | tf_op jit(solution)/shard_map/all_to_all | solution.py:529
  565.7 30.2 %copy-start.2 = (f32[512,1536]{1,0:T(8,128)S(1)}, f32[512,1536]{1,0:T(8,128)}, u32[]{:S(2)}) copy-start(f32[512,1536]{1,0:T(8,128)} %copy-done.1) | copy-start | bytes 9437188
  595.9 30.9 %copy-start.52 = (f32[192,256]{0,1:T(8,128)S(1)}, f32[192,256]{0,1:T(8,128)}, u32[]{:S(2)}) copy-start(f32[192,256]{0,1:T(8,128)} %copy.253) | copy-start | bytes 589828
  (127 other events, 521.7 us)
Sparse Core Ops, SparseCore 0:
  11.5 46.4 all-gather.4
  60.4 28.8 all-gather.6
  141.2 39.5 reduce-scatter.12
  185.1 41.4 reduce-scatter.14
  229.8 42.3 reduce-scatter.16
  298.3 44.4 all-reduce.35
  344.7 58.5 all-gather.8
  406.5 36.6 reduce-scatter.18
  446.2 131.7 all-reduce.37
